TPU v7x, 512 devices: a whole 4x8x8 slice. The times are simulated.
512 devices in a mesh: row: 32 (over z, y_lo, core), col: 16 (over x, y_hi).
Axes of the slice: x: 4, y: 8 (y_hi: 4, y_lo: 2; y = y_hi * 2 + y_lo), z: 8, core: 2. Of those that a mesh axis runs over, the one named last changes fastest.
Arguments:
- view_a: float32 [128, 512, 768], P('col', 'row'), may hold values from 0.25 to 4
- view_b: float32 [128, 768, 512], P('col', 'row'), may hold values from 0.25 to 4
- estimate: float32 [128, 512, 768], P('col', 'row'), may hold values from 0.5 to 2
- axial_kernel: float32 [2, 31], replicated, may hold values from 0.05 to 1
- lateral_kernel: float32 [2, 2, 11], replicated, may hold values from 0.05 to 1
Outputs:
- restored: float32 [128, 512, 768], P('col', 'row')
All inputs are finite; a program needn't handle non-finite values.
Results may differ from a plain program's by a relative error of at most 0.00002.
Values sent between devices are 32-bit elements; how exact they have to be, the bound alone decides.
No kernel may reach another device: no remote copies, remote signals or barrier semaphores. Data moves between devices by JAX's collectives and lax.ppermute only.
A program may use at most 64 MiB of HBM per device.

v0:
```python
import jax
import jax.numpy as jnp
from jax import lax
from jax.sharding import PartitionSpec as P

ITERS = 2


def padded_2(block, sides, width):
    for axis, dim in sides:
        count = lax.axis_size(axis)
        forward = [(i, i + 1) for i in range(count - 1)]
        backward = [(target, source) for source, target in forward]
        low = lax.ppermute(
            lax.slice_in_dim(block, block.shape[dim] - width, None, axis=dim), axis, forward
        )
        high = lax.ppermute(lax.slice_in_dim(block, 0, width, axis=dim), axis, backward)
        block = jnp.concatenate([low, block, high], axis=dim)
    return block


def weigh(padded, weights, dimension, extent):
    summed = weights[0] * lax.slice_in_dim(padded, 0, extent, axis=dimension)
    for offset in range(1, weights.shape[0]):
        summed = summed + weights[offset] * lax.slice_in_dim(
            padded, offset, offset + extent, axis=dimension
        )
    return summed


def blur_dim(volume, weights, dimension):
    margin = weights.shape[0] // 2
    extent = volume.shape[dimension]
    if dimension == 2:
        padded = jnp.pad(volume, ((0, 0), (0, 0), (margin, margin)))
    elif dimension == 1:
        padded = padded_2(volume, (("row", 1),), margin)
    else:
        padded = padded_2(volume, (("col", 0),), margin)
    return weigh(padded, weights, dimension, extent)


def project(volume, in_plane, axial_weights, depth_weights, plane_dim, axial_dim):
    volume = blur_dim(volume, in_plane, plane_dim)
    volume = blur_dim(volume, axial_weights, axial_dim)
    return blur_dim(volume, depth_weights, 0)


def reframe(volume):
    arrived = lax.all_to_all(volume, "row", split_axis=2, concat_axis=1, tiled=True)
    return jnp.swapaxes(arrived, 1, 2)


def update_a(estimate, view_a, axial, lateral):
    blurred = project(estimate, lateral[0, 1], axial[0], lateral[0, 0], 2, 1)
    quotient = view_a / blurred
    return estimate * project(
        quotient, lateral[0, 1][::-1], axial[0][::-1], lateral[0, 0][::-1], 2, 1
    )


def per_device(view_a, view_b, estimate, axial_kernel, lateral_kernel):
    axial = axial_kernel / jnp.sum(axial_kernel, axis=1, keepdims=True)
    lateral = lateral_kernel / jnp.sum(lateral_kernel, axis=2, keepdims=True)
    for iteration in range(ITERS):
        estimate = update_a(estimate, view_a, axial, lateral)
        turned = reframe(estimate)
        blurred = project(turned, lateral[1, 1], axial[1], lateral[1, 0], 2, 1)
        quotient = view_b / blurred
        correction = project(
            quotient, lateral[1, 1][::-1], axial[1][::-1], lateral[1, 0][::-1], 2, 1
        )
        estimate = estimate * reframe(correction)
    return estimate


def solution(mesh):
    in_specs = (P("col", "row", None), P("col", "row", None), P("col", "row", None), P(), P())
    out_specs = P("col", "row", None)
    return jax.shard_map(
        per_device, mesh=mesh, in_specs=in_specs, out_specs=out_specs, check_vma=False
    )
```

profile of v0, /device:TPU:58, one launch (start us, length us, event | category | flops | bytes accessed | tf_op | source)
XLA Modules:
  0.0 694.7 jit_solution(2831640452632077989)
XLA Ops:
  2.9 11.5 %fusion.10 = f32[8,16,768]{2,1,0:T(8,128)S(1)} fusion(f32[8,16,768]{2,1,0:T(8,128)} %param.7, f32[]{:T(128)} %bitcast.14, f32[]{:T(128)} %bitcast.13, f32[]{:T(128)} %bitcast.12, f32[]{:T(128)} %bitcast.11, f32[]{:T(128)} %bitcast.10, f32[]{:T(128)} %bitcast.9, f32[]{:T(128)} %bitcast.8, f32[]{:T(128)} %bitcast.7, f32[]{:T(128)} %bitcast.6, f32[]{:T(128)} %bitcast.5, ...), kind=kLoop, calls=%fused_computation.666 | loop fusion | flops 2064384 | bytes 786476 | tf_op jit(solution)/shard_map/add | solution.py:25
  16.4 3.6 collective-permute-start.1
  23.7 4.7 collective-permute-done.1
  28.5 21.6 %fusion.979 = f32[8,16,768]{2,1,0:T(8,128)S(1)} fusion(f32[8,16,768]{2,1,0:T(8,128)S(1)} %fusion.10, f32[8,15,768]{2,1,0:T(8,128)S(1)} %collective-permute-done.1, f32[8,15,768]{2,1,0:T(8,128)S(1)} %collective-permute-done, f32[]{:T(128)} %bitcast.43, f32[]{:T(128)} %bitcast.42, f32[]{:T(128)} %bitcast.41, f32[]{:T(128)} %bitcast.40, f32[]{:T(128)} %bitcast.39, ...), kind=kLoop, calls=%fused_computation.1635 | loop fusion | flops 8945664 | bytes 1523836 | tf_op jit(solution)/shard_map/add | solution.py:25
  52.9 4.0 collective-permute-start.3
  56.9 7.3 %collective-permute-done.2 = f32[5,16,768]{2,1,0:T(8,128)S(1)} collective-permute-done((f32[5,16,768]{2,1,0:T(8,128)S(1)}, f32[5,16,768]{2,1,0:T(8,128)S(1)}, u32[]{:S(2)}, u32[]{:S(2)}) %collective-permute-start.2) | collective-permute-done | bytes 245792 | tf_op jit(solution)/shard_map/ppermute | solution.py:14
  67.2 7.1 %fusion.351 = f32[8,16,768]{2,1,0:T(8,128)S(1)} fusion(f32[8,16,768]{2,1,0:T(8,128)S(1)} %copy-done.1, f32[8,16,768]{2,1,0:T(8,128)S(1)} %fusion.979, f32[5,16,768]{2,1,0:T(8,128)S(1)} %collective-permute-done.3, f32[5,16,768]{2,1,0:T(8,128)S(1)} %collective-permute-done.2, f32[]{:T(128)} %bitcast.52, f32[]{:T(128)} %bitcast.51, f32[]{:T(128)} %bitcast.50, ...), kind=kLoop, calls=%fused_computation.1007 | loop fusion | flops 3145728 | bytes 1671212 | tf_op jit(solution)/shard_map/div | solution.py:56
  74.3 8.0 %fusion.30 = f32[8,16,768]{2,1,0:T(8,128)S(1)} fusion(f32[8,16,768]{2,1,0:T(8,128)S(1)} %fusion.351, f32[]{:T(128)} %bitcast.14, f32[]{:T(128)} %bitcast.13, f32[]{:T(128)} %bitcast.12, f32[]{:T(128)} %bitcast.11, f32[]{:T(128)} %bitcast.10, f32[]{:T(128)} %bitcast.9, f32[]{:T(128)} %bitcast.8, f32[]{:T(128)} %bitcast.7, f32[]{:T(128)} %bitcast.6, ...), kind=kLoop, calls=%fused_computation.686 | loop fusion | flops 2064384 | bytes 786476 | tf_op jit(solution)/shard_map/add | solution.py:25
  84.7 4.0 collective-permute-start.5
  95.7 21.6 %fusion.893 = f32[8,16,768]{2,1,0:T(8,128)S(1)} fusion(f32[8,16,768]{2,1,0:T(8,128)S(1)} %fusion.30, f32[8,15,768]{2,1,0:T(8,128)S(1)} %collective-permute-done.5, f32[8,15,768]{2,1,0:T(8,128)S(1)} %collective-permute-done.4, f32[]{:T(128)} %bitcast.43, f32[]{:T(128)} %bitcast.42, f32[]{:T(128)} %bitcast.41, f32[]{:T(128)} %bitcast.40, f32[]{:T(128)} %bitcast.39, ...), kind=kLoop, calls=%fused_computation.1549 | loop fusion | flops 8945664 | bytes 1523836 | tf_op jit(solution)/shard_map/add | solution.py:25
  117.4 5.1 collective-permute-start.6
  124.5 6.4 collective-permute-done.6
  130.8 4.4 collective-permute-done.7
  135.2 7.0 %fusion.324 = f32[8,16,768]{2,1,0:T(8,128)S(1)} fusion(f32[8,16,768]{2,1,0:T(8,128)S(1)} %copy-done, f32[8,16,768]{2,1,0:T(8,128)S(1)} %fusion.893, f32[5,16,768]{2,1,0:T(8,128)S(1)} %collective-permute-done.7, f32[5,16,768]{2,1,0:T(8,128)S(1)} %collective-permute-done.6, f32[]{:T(128)} %bitcast.52, f32[]{:T(128)} %bitcast.51, f32[]{:T(128)} %bitcast.50, ...), kind=kLoop, calls=%fused_computation.980 | loop fusion | flops 3145728 | bytes 1671212 | tf_op jit(solution)/shard_map/mul | solution.py:57
  145.4 18.7 %all-to-all-start = ((f32[32,1,3072]{2,1,0:T(1,128)}), f32[32,1,3072]{2,1,0:T(1,128)S(1)}, u32[]{:S(2)}, u32[]{:S(2)}) async-start(f32[32,1,3072]{2,1,0:T(1,128)} %reshape.426), calls=%async_computation | async-start | bytes 786432 | tf_op jit(solution)/shard_map/all_to_all | solution.py:50
  164.9 14.0 %all-to-all-done = f32[32,1,3072]{2,1,0:T(1,128)S(1)} async-done(((f32[32,1,3072]{2,1,0:T(1,128)}), f32[32,1,3072]{2,1,0:T(1,128)S(1)}, u32[]{:S(2)}, u32[]{:S(2)}) %all-to-all-start) | async-done | bytes 393248 | tf_op jit(solution)/shard_map/all_to_all | solution.py:50
  187.4 3.7 all_to_all.55
  191.1 8.0 %fusion.90 = f32[8,24,512]{2,1,0:T(8,128)S(1)} fusion(f32[8,24,512]{2,1,0:T(8,128)S(1)} %bitcast.160, f32[]{:T(128)} %bitcast.71, f32[]{:T(128)} %bitcast.70, f32[]{:T(128)} %bitcast.69, f32[]{:T(128)} %bitcast.68, f32[]{:T(128)} %bitcast.67, f32[]{:T(128)} %bitcast.66, f32[]{:T(128)} %bitcast.65, f32[]{:T(128)} %bitcast.64, f32[]{:T(128)} %bitcast.63, ...), kind=kLoop, calls=%fused_computation.746 | loop fusion | flops 2064384 | bytes 786476 | tf_op jit(solution)/shard_map/add | solution.py:25
  201.1 3.6 collective-permute-start.9
  208.6 21.3 %fusion.635 = f32[8,24,512]{2,1,0:T(8,128)S(1)} fusion(f32[8,24,512]{2,1,0:T(8,128)S(1)} %fusion.90, f32[8,15,512]{2,1,0:T(8,128)S(1)} %collective-permute-done.9, f32[8,15,512]{2,1,0:T(8,128)S(1)} %collective-permute-done.8, f32[]{:T(128)} %bitcast.100, f32[]{:T(128)} %bitcast.99, f32[]{:T(128)} %bitcast.98, f32[]{:T(128)} %bitcast.97, f32[]{:T(128)} %bitcast.96, ...), kind=kLoop, calls=%fused_computation.1291 | loop fusion | flops 8945664 | bytes 1278076 | tf_op jit(solution)/shard_map/add | solution.py:25
  233.1 3.6 collective-permute-start.11
  236.7 6.5 collective-permute-done.10
  243.2 4.6 collective-permute-done.11
  247.8 7.1 %fusion.297 = f32[8,24,512]{2,1,0:T(8,128)S(1)} fusion(f32[8,24,512]{2,1,0:T(8,128)S(1)} %copy-done.3, f32[8,24,512]{2,1,0:T(8,128)S(1)} %fusion.635, f32[5,24,512]{2,1,0:T(8,128)S(1)} %collective-permute-done.11, f32[5,24,512]{2,1,0:T(8,128)S(1)} %collective-permute-done.10, f32[]{:T(128)} %bitcast.109, f32[]{:T(128)} %bitcast.108, f32[]{:T(128)} %bitcast.107, ...), kind=kLoop, calls=%fused_computation.953 | loop fusion | flops 3145728 | bytes 1671212 | tf_op jit(solution)/shard_map/div | solution.py:69
  254.8 8.0 %fusion.110 = f32[8,24,512]{2,1,0:T(8,128)S(1)} fusion(f32[8,24,512]{2,1,0:T(8,128)S(1)} %fusion.297, f32[]{:T(128)} %bitcast.71, f32[]{:T(128)} %bitcast.70, f32[]{:T(128)} %bitcast.69, f32[]{:T(128)} %bitcast.68, f32[]{:T(128)} %bitcast.67, f32[]{:T(128)} %bitcast.66, f32[]{:T(128)} %bitcast.65, f32[]{:T(128)} %bitcast.64, f32[]{:T(128)} %bitcast.63, ...), kind=kLoop, calls=%fused_computation.766 | loop fusion | flops 2064384 | bytes 786476 | tf_op jit(solution)/shard_map/add | solution.py:25
  264.9 4.0 collective-permute-start.13
  271.0 4.0 collective-permute-done.13
  275.0 21.3 %fusion.549 = f32[8,24,512]{2,1,0:T(8,128)S(1)} fusion(f32[8,24,512]{2,1,0:T(8,128)S(1)} %fusion.110, f32[8,15,512]{2,1,0:T(8,128)S(1)} %collective-permute-done.13, f32[8,15,512]{2,1,0:T(8,128)S(1)} %collective-permute-done.12, f32[]{:T(128)} %bitcast.100, f32[]{:T(128)} %bitcast.99, f32[]{:T(128)} %bitcast.98, f32[]{:T(128)} %bitcast.97, f32[]{:T(128)} %bitcast.96, ...), kind=kLoop, calls=%fused_computation.1205 | loop fusion | flops 8945664 | bytes 1278076 | tf_op jit(solution)/shard_map/add | solution.py:25
  298.9 4.3 collective-permute-start.15
  303.3 6.3 collective-permute-done.14
  309.5 4.5 collective-permute-done.15
  314.0 7.0 %fusion.270 = f32[8,24,512]{2,1,0:T(8,128)S(1)} fusion(f32[8,24,512]{2,1,0:T(8,128)S(1)} %fusion.549, f32[5,24,512]{2,1,0:T(8,128)S(1)} %collective-permute-done.15, f32[5,24,512]{2,1,0:T(8,128)S(1)} %collective-permute-done.14, f32[]{:T(128)} %bitcast.109, f32[]{:T(128)} %bitcast.108, f32[]{:T(128)} %bitcast.107, f32[]{:T(128)} %bitcast.106, f32[]{:T(128)} %bitcast.105, ...), kind=kLoop, calls=%fused_computation.926 | loop fusion | flops 3047424 | bytes 1277996 | tf_op jit(solution)/shard_map/add | solution.py:25
  323.5 22.7 %all_to_all.72 = f32[32,1,3072]{2,1,0:T(1,128)S(1)} all-to-all(f32[32,1,3072]{2,1,0:T(1,128)S(1)} %reshape.428), channel_id=1, replica_groups=mesh['row'=32,'col'=16] {'row'}, dimensions={0} | all-to-all | bytes 786432 | tf_op jit(solution)/shard_map/all_to_all | solution.py:50
  354.7 8.0 %fusion.50 = f32[8,16,768]{2,1,0:T(8,128)S(1)} fusion(f32[8,16,768]{2,1,0:T(8,128)S(1)} %bitcast_multiply_fusion.1, f32[]{:T(128)} %bitcast.14, f32[]{:T(128)} %bitcast.13, f32[]{:T(128)} %bitcast.12, f32[]{:T(128)} %bitcast.11, f32[]{:T(128)} %bitcast.10, f32[]{:T(128)} %bitcast.9, f32[]{:T(128)} %bitcast.8, f32[]{:T(128)} %bitcast.7, f32[]{:T(128)} %bitcast.6, ...), kind=kLoop, calls=%fused_computation.706 | loop fusion | flops 2064384 | bytes 786476 | tf_op jit(solution)/shard_map/add | solution.py:25
  364.7 3.6 collective-permute-start.17
  374.2 21.6 %fusion.807 = f32[8,16,768]{2,1,0:T(8,128)S(1)} fusion(f32[8,16,768]{2,1,0:T(8,128)S(1)} %fusion.50, f32[8,15,768]{2,1,0:T(8,128)S(1)} %collective-permute-done.17, f32[8,15,768]{2,1,0:T(8,128)S(1)} %collective-permute-done.16, f32[]{:T(128)} %bitcast.43, f32[]{:T(128)} %bitcast.42, f32[]{:T(128)} %bitcast.41, f32[]{:T(128)} %bitcast.40, f32[]{:T(128)} %bitcast.39, ...), kind=kLoop, calls=%fused_computation.1463 | loop fusion | flops 8945664 | bytes 1523836 | tf_op jit(solution)/shard_map/add | solution.py:25
  399.0 3.6 collective-permute-start.19
  402.6 6.6 collective-permute-done.18
  409.3 5.4 collective-permute-done.19
  414.7 7.1 %fusion.244 = f32[8,16,768]{2,1,0:T(8,128)S(1)} fusion(f32[8,16,768]{2,1,0:T(8,128)S(1)} %copy-done.2, f32[8,16,768]{2,1,0:T(8,128)S(1)} %fusion.807, f32[5,16,768]{2,1,0:T(8,128)S(1)} %collective-permute-done.19, f32[5,16,768]{2,1,0:T(8,128)S(1)} %collective-permute-done.18, f32[]{:T(128)} %bitcast.52, f32[]{:T(128)} %bitcast.51, f32[]{:T(128)} %bitcast.50, ...), kind=kLoop, calls=%fused_computation.900 | loop fusion | flops 3145728 | bytes 1671212 | tf_op jit(solution)/shard_map/div | solution.py:56
  421.8 8.0 %fusion.70 = f32[8,16,768]{2,1,0:T(8,128)S(1)} fusion(f32[8,16,768]{2,1,0:T(8,128)S(1)} %fusion.244, f32[]{:T(128)} %bitcast.14, f32[]{:T(128)} %bitcast.13, f32[]{:T(128)} %bitcast.12, f32[]{:T(128)} %bitcast.11, f32[]{:T(128)} %bitcast.10, f32[]{:T(128)} %bitcast.9, f32[]{:T(128)} %bitcast.8, f32[]{:T(128)} %bitcast.7, f32[]{:T(128)} %bitcast.6, ...), kind=kLoop, calls=%fused_computation.726 | loop fusion | flops 2064384 | bytes 786476 | tf_op jit(solution)/shard_map/add | solution.py:25
  439.0 5.6 collective-permute-done.21
  444.6 21.6 %fusion.721 = f32[8,16,768]{2,1,0:T(8,128)S(1)} fusion(f32[8,16,768]{2,1,0:T(8,128)S(1)} %fusion.70, f32[8,15,768]{2,1,0:T(8,128)S(1)} %collective-permute-done.21, f32[8,15,768]{2,1,0:T(8,128)S(1)} %collective-permute-done.20, f32[]{:T(128)} %bitcast.43, f32[]{:T(128)} %bitcast.42, f32[]{:T(128)} %bitcast.41, f32[]{:T(128)} %bitcast.40, f32[]{:T(128)} %bitcast.39, ...), kind=kLoop, calls=%fused_computation.1377 | loop fusion | flops 8945664 | bytes 1523836 | tf_op jit(solution)/shard_map/add | solution.py:25
  468.5 4.6 collective-permute-start.23
  473.0 7.0 %collective-permute-done.22 = f32[5,16,768]{2,1,0:T(8,128)S(1)} collective-permute-done((f32[5,16,768]{2,1,0:T(8,128)S(1)}, f32[5,16,768]{2,1,0:T(8,128)S(1)}, u32[]{:S(2)}, u32[]{:S(2)}) %collective-permute-start.22) | collective-permute-done | bytes 245792 | tf_op jit(solution)/shard_map/ppermute | solution.py:14
  480.0 3.7 collective-permute-done.23
  483.7 7.0 %fusion.217 = f32[8,16,768]{2,1,0:T(8,128)S(1)} fusion(f32[8,16,768]{2,1,0:T(8,128)S(1)} %bitcast_multiply_fusion.1, f32[8,16,768]{2,1,0:T(8,128)S(1)} %fusion.721, f32[5,16,768]{2,1,0:T(8,128)S(1)} %collective-permute-done.23, f32[5,16,768]{2,1,0:T(8,128)S(1)} %collective-permute-done.22, f32[]{:T(128)} %bitcast.52, f32[]{:T(128)} %bitcast.51, ...), kind=kLoop, calls=%fused_computation.873 | loop fusion | flops 3145728 | bytes 1671212 | tf_op jit(solution)/shard_map/mul | solution.py:57
  493.9 24.3 %all_to_all.73 = f32[32,1,3072]{2,1,0:T(1,128)S(1)} all-to-all(f32[32,1,3072]{2,1,0:T(1,128)} %reshape.430), channel_id=1, replica_groups=mesh['row'=32,'col'=16] {'row'}, dimensions={0} | all-to-all | bytes 786432 | tf_op jit(solution)/shard_map/all_to_all | solution.py:50
  526.2 3.7 all_to_all.63
  529.8 8.0 %fusion.130 = f32[8,24,512]{2,1,0:T(8,128)S(1)} fusion(f32[8,24,512]{2,1,0:T(8,128)S(1)} %bitcast.161, f32[]{:T(128)} %bitcast.71, f32[]{:T(128)} %bitcast.70, f32[]{:T(128)} %bitcast.69, f32[]{:T(128)} %bitcast.68, f32[]{:T(128)} %bitcast.67, f32[]{:T(128)} %bitcast.66, f32[]{:T(128)} %bitcast.65, f32[]{:T(128)} %bitcast.64, f32[]{:T(128)} %bitcast.63, ...), kind=kLoop, calls=%fused_computation.786 | loop fusion | flops 2064384 | bytes 786476 | tf_op jit(solution)/shard_map/add | solution.py:25
  539.8 3.6 collective-permute-start.25
  547.3 21.3 %fusion.463 = f32[8,24,512]{2,1,0:T(8,128)S(1)} fusion(f32[8,24,512]{2,1,0:T(8,128)S(1)} %fusion.130, f32[8,15,512]{2,1,0:T(8,128)S(1)} %collective-permute-done.25, f32[8,15,512]{2,1,0:T(8,128)S(1)} %collective-permute-done.24, f32[]{:T(128)} %bitcast.100, f32[]{:T(128)} %bitcast.99, f32[]{:T(128)} %bitcast.98, f32[]{:T(128)} %bitcast.97, f32[]{:T(128)} %bitcast.96, ...), kind=kLoop, calls=%fused_computation.1119 | loop fusion | flops 8945664 | bytes 1278076 | tf_op jit(solution)/shard_map/add | solution.py:25
  571.6 3.9 collective-permute-start.27
  575.4 6.7 collective-permute-done.26
  582.1 5.0 collective-permute-done.27
  587.0 7.1 %fusion.190 = f32[8,24,512]{2,1,0:T(8,128)S(1)} fusion(f32[8,24,512]{2,1,0:T(8,128)S(1)} %copy-done.4, f32[8,24,512]{2,1,0:T(8,128)S(1)} %fusion.463, f32[5,24,512]{2,1,0:T(8,128)S(1)} %collective-permute-done.27, f32[5,24,512]{2,1,0:T(8,128)S(1)} %collective-permute-done.26, f32[]{:T(128)} %bitcast.109, f32[]{:T(128)} %bitcast.108, f32[]{:T(128)} %bitcast.107, ...), kind=kLoop, calls=%fused_computation.846 | loop fusion | flops 3145728 | bytes 1671212 | tf_op jit(solution)/shard_map/div | solution.py:69
  594.1 8.0 %fusion.150 = f32[8,24,512]{2,1,0:T(8,128)S(1)} fusion(f32[8,24,512]{2,1,0:T(8,128)S(1)} %fusion.190, f32[]{:T(128)} %bitcast.71, f32[]{:T(128)} %bitcast.70, f32[]{:T(128)} %bitcast.69, f32[]{:T(128)} %bitcast.68, f32[]{:T(128)} %bitcast.67, f32[]{:T(128)} %bitcast.66, f32[]{:T(128)} %bitcast.65, f32[]{:T(128)} %bitcast.64, f32[]{:T(128)} %bitcast.63, ...), kind=kLoop, calls=%fused_computation.806 | loop fusion | flops 2064384 | bytes 786476 | tf_op jit(solution)/shard_map/add | solution.py:25
  609.8 4.4 collective-permute-done.29
  614.2 21.3 %fusion.377 = f32[8,24,512]{2,1,0:T(8,128)S(1)} fusion(f32[8,24,512]{2,1,0:T(8,128)S(1)} %fusion.150, f32[8,15,512]{2,1,0:T(8,128)S(1)} %collective-permute-done.29, f32[8,15,512]{2,1,0:T(8,128)S(1)} %collective-permute-done.28, f32[]{:T(128)} %bitcast.100, f32[]{:T(128)} %bitcast.99, f32[]{:T(128)} %bitcast.98, f32[]{:T(128)} %bitcast.97, f32[]{:T(128)} %bitcast.96, ...), kind=kLoop, calls=%fused_computation.1033 | loop fusion | flops 8945664 | bytes 1278076 | tf_op jit(solution)/shard_map/add | solution.py:25
  638.2 4.3 collective-permute-start.31
  642.5 5.3 collective-permute-done.30
  647.8 5.5 collective-permute-done.31
  653.2 7.0 %fusion.163 = f32[8,24,512]{2,1,0:T(8,128)S(1)} fusion(f32[8,24,512]{2,1,0:T(8,128)S(1)} %fusion.377, f32[5,24,512]{2,1,0:T(8,128)S(1)} %collective-permute-done.31, f32[5,24,512]{2,1,0:T(8,128)S(1)} %collective-permute-done.30, f32[]{:T(128)} %bitcast.109, f32[]{:T(128)} %bitcast.108, f32[]{:T(128)} %bitcast.107, f32[]{:T(128)} %bitcast.106, f32[]{:T(128)} %bitcast.105, ...), kind=kLoop, calls=%fused_computation.819 | loop fusion | flops 3047424 | bytes 1277996 | tf_op jit(solution)/shard_map/add | solution.py:25
  662.7 22.6 %all_to_all.74 = f32[32,1,3072]{2,1,0:T(1,128)S(1)} all-to-all(f32[32,1,3072]{2,1,0:T(1,128)S(1)} %reshape.432), channel_id=1, replica_groups=mesh['row'=32,'col'=16] {'row'}, dimensions={0} | all-to-all | bytes 786432 | tf_op jit(solution)/shard_map/all_to_all | solution.py:50
  (93 shorter events, 129.0 us)
Async XLA Ops:
  0.0 67.2 %copy-start.1 = (f32[8,16,768]{2,1,0:T(8,128)S(1)}, f32[8,16,768]{2,1,0:T(8,128)}, u32[]{:S(2)}) copy-start(f32[8,16,768]{2,1,0:T(8,128)} %param.5) | copy-start | bytes 1179652
  14.5 9.2 %collective-permute-start = (f32[8,15,768]{2,1,0:T(8,128)S(1)}, f32[8,15,768]{2,1,0:T(8,128)S(1)}, u32[]{:S(2)}, u32[]{:S(2)}) collective-permute-start(f32[8,15,768]{2,1,0:T(8,128)S(1)} %get-tuple-element.35), channel_id=1, source_target_pairs={{0,16},{16,32},{32,48},{48,64},{64,80},{80,96},{96,112},{112,128},... | collective-permute-start | bytes 1105928 | tf_op jit(solution)/shard_map/ppermute | solution.py:14
  16.4 12.1 %collective-permute-start.1 = (f32[8,15,768]{2,1,0:T(8,128)S(1)}, f32[8,15,768]{2,1,0:T(8,128)S(1)}, u32[]{:S(2)}, u32[]{:S(2)}) collective-permute-start(f32[8,15,768]{2,1,0:T(8,128)S(1)} %get-tuple-element.36), channel_id=1, source_target_pairs={{16,0},{32,16},{48,32},{64,48},{80,64},{96,80},{112,96},{128,112},... | collective-permute-start | bytes 1105928 | tf_op jit(solution)/shard_map/ppermute | solution.py:17
  50.1 14.0 %collective-permute-start.2 = (f32[5,16,768]{2,1,0:T(8,128)S(1)}, f32[5,16,768]{2,1,0:T(8,128)S(1)}, u32[]{:S(2)}, u32[]{:S(2)}) collective-permute-start(f32[5,16,768]{2,1,0:T(8,128)S(1)} %get-tuple-element.33), channel_id=1, source_target_pairs={{0,1},{1,2},{2,3},{3,4},{4,5},{5,6},{6,7},{7,8},{8,9},{9,10},{10,1... | collective-permute-start | bytes 737288 | tf_op jit(solution)/shard_map/ppermute | solution.py:14
  52.9 14.3 %collective-permute-start.3 = (f32[5,16,768]{2,1,0:T(8,128)S(1)}, f32[5,16,768]{2,1,0:T(8,128)S(1)}, u32[]{:S(2)}, u32[]{:S(2)}) collective-permute-start(f32[5,16,768]{2,1,0:T(8,128)S(1)} %get-tuple-element.34), channel_id=1, source_target_pairs={{1,0},{2,1},{3,2},{4,3},{5,4},{6,5},{7,6},{8,7},{9,8},{10,9},{11,1... | collective-permute-start | bytes 737288 | tf_op jit(solution)/shard_map/ppermute | solution.py:17
  67.2 68.0 %copy-start = (f32[8,16,768]{2,1,0:T(8,128)S(1)}, f32[8,16,768]{2,1,0:T(8,128)}, u32[]{:S(2)}) copy-start(f32[8,16,768]{2,1,0:T(8,128)} %param.7) | copy-start | bytes 1179652
  82.4 9.9 %collective-permute-start.4 = (f32[8,15,768]{2,1,0:T(8,128)S(1)}, f32[8,15,768]{2,1,0:T(8,128)S(1)}, u32[]{:S(2)}, u32[]{:S(2)}) collective-permute-start(f32[8,15,768]{2,1,0:T(8,128)S(1)} %get-tuple-element.31), channel_id=1, source_target_pairs={{0,16},{16,32},{32,48},{48,64},{64,80},{80,96},{96,112},{112,128},... | collective-permute-start | bytes 1105928 | tf_op jit(solution)/shard_map/ppermute | solution.py:14
  84.7 11.0 %collective-permute-start.5 = (f32[8,15,768]{2,1,0:T(8,128)S(1)}, f32[8,15,768]{2,1,0:T(8,128)S(1)}, u32[]{:S(2)}, u32[]{:S(2)}) collective-permute-start(f32[8,15,768]{2,1,0:T(8,128)S(1)} %get-tuple-element.32), channel_id=1, source_target_pairs={{16,0},{32,16},{48,32},{64,48},{80,64},{96,80},{112,96},{128,112},... | collective-permute-start | bytes 1105928 | tf_op jit(solution)/shard_map/ppermute | solution.py:17
  117.4 13.5 %collective-permute-start.6 = (f32[5,16,768]{2,1,0:T(8,128)S(1)}, f32[5,16,768]{2,1,0:T(8,128)S(1)}, u32[]{:S(2)}, u32[]{:S(2)}) collective-permute-start(f32[5,16,768]{2,1,0:T(8,128)S(1)} %get-tuple-element.29), channel_id=1, source_target_pairs={{0,1},{1,2},{2,3},{3,4},{4,5},{5,6},{6,7},{7,8},{8,9},{9,10},{10,1... | collective-permute-start | bytes 737288 | tf_op jit(solution)/shard_map/ppermute | solution.py:14
  122.5 12.7 %collective-permute-start.7 = (f32[5,16,768]{2,1,0:T(8,128)S(1)}, f32[5,16,768]{2,1,0:T(8,128)S(1)}, u32[]{:S(2)}, u32[]{:S(2)}) collective-permute-start(f32[5,16,768]{2,1,0:T(8,128)S(1)} %get-tuple-element.30), channel_id=1, source_target_pairs={{1,0},{2,1},{3,2},{4,3},{5,4},{6,5},{7,6},{8,7},{9,8},{10,9},{11,1... | collective-permute-start | bytes 737288 | tf_op jit(solution)/shard_map/ppermute | solution.py:17
  145.4 33.5 %all-to-all-start = ((f32[32,1,3072]{2,1,0:T(1,128)}), f32[32,1,3072]{2,1,0:T(1,128)S(1)}, u32[]{:S(2)}, u32[]{:S(2)}) async-start(f32[32,1,3072]{2,1,0:T(1,128)} %reshape.426), calls=%async_computation | async-start | bytes 786432 | tf_op jit(solution)/shard_map/all_to_all | solution.py:50
  187.4 60.4 %copy-start.3 = (f32[8,24,512]{2,1,0:T(8,128)S(1)}, f32[8,24,512]{2,1,0:T(8,128)}, u32[]{:S(2)}) copy-start(f32[8,24,512]{2,1,0:T(8,128)} %param.6) | copy-start | bytes 1179652
  199.1 7.7 %collective-permute-start.8 = (f32[8,15,512]{2,1,0:T(8,128)S(1)}, f32[8,15,512]{2,1,0:T(8,128)S(1)}, u32[]{:S(2)}, u32[]{:S(2)}) collective-permute-start(f32[8,15,512]{2,1,0:T(8,128)S(1)} %get-tuple-element.27), channel_id=1, source_target_pairs={{0,16},{16,32},{32,48},{48,64},{64,80},{80,96},{96,112},{112,128},... | collective-permute-start | bytes 737288 | tf_op jit(solution)/shard_map/ppermute | solution.py:14
  201.1 7.5 %collective-permute-start.9 = (f32[8,15,512]{2,1,0:T(8,128)S(1)}, f32[8,15,512]{2,1,0:T(8,128)S(1)}, u32[]{:S(2)}, u32[]{:S(2)}) collective-permute-start(f32[8,15,512]{2,1,0:T(8,128)S(1)} %get-tuple-element.28), channel_id=1, source_target_pairs={{16,0},{32,16},{48,32},{64,48},{80,64},{96,80},{112,96},{128,112},... | collective-permute-start | bytes 737288 | tf_op jit(solution)/shard_map/ppermute | solution.py:17
  229.9 13.3 %collective-permute-start.10 = (f32[5,24,512]{2,1,0:T(8,128)S(1)}, f32[5,24,512]{2,1,0:T(8,128)S(1)}, u32[]{:S(2)}, u32[]{:S(2)}) collective-permute-start(f32[5,24,512]{2,1,0:T(8,128)S(1)} %get-tuple-element.25), channel_id=1, source_target_pairs={{0,1},{1,2},{2,3},{3,4},{4,5},{5,6},{6,7},{7,8},{8,9},{9,10},{10,1... | collective-permute-start | bytes 737288 | tf_op jit(solution)/shard_map/ppermute | solution.py:14
  233.1 14.7 %collective-permute-start.11 = (f32[5,24,512]{2,1,0:T(8,128)S(1)}, f32[5,24,512]{2,1,0:T(8,128)S(1)}, u32[]{:S(2)}, u32[]{:S(2)}) collective-permute-start(f32[5,24,512]{2,1,0:T(8,128)S(1)} %get-tuple-element.26), channel_id=1, source_target_pairs={{1,0},{2,1},{3,2},{4,3},{5,4},{6,5},{7,6},{8,7},{9,8},{10,9},{11,1... | collective-permute-start | bytes 737288 | tf_op jit(solution)/shard_map/ppermute | solution.py:17
  262.9 8.1 %collective-permute-start.12 = (f32[8,15,512]{2,1,0:T(8,128)S(1)}, f32[8,15,512]{2,1,0:T(8,128)S(1)}, u32[]{:S(2)}, u32[]{:S(2)}) collective-permute-start(f32[8,15,512]{2,1,0:T(8,128)S(1)} %get-tuple-element.23), channel_id=1, source_target_pairs={{0,16},{16,32},{32,48},{48,64},{64,80},{80,96},{96,112},{112,128},... | collective-permute-start | bytes 737288 | tf_op jit(solution)/shard_map/ppermute | solution.py:14
  264.9 10.1 %collective-permute-start.13 = (f32[8,15,512]{2,1,0:T(8,128)S(1)}, f32[8,15,512]{2,1,0:T(8,128)S(1)}, u32[]{:S(2)}, u32[]{:S(2)}) collective-permute-start(f32[8,15,512]{2,1,0:T(8,128)S(1)} %get-tuple-element.24), channel_id=1, source_target_pairs={{16,0},{32,16},{48,32},{64,48},{80,64},{96,80},{112,96},{128,112},... | collective-permute-start | bytes 737288 | tf_op jit(solution)/shard_map/ppermute | solution.py:17
  296.3 13.2 %collective-permute-start.14 = (f32[5,24,512]{2,1,0:T(8,128)S(1)}, f32[5,24,512]{2,1,0:T(8,128)S(1)}, u32[]{:S(2)}, u32[]{:S(2)}) collective-permute-start(f32[5,24,512]{2,1,0:T(8,128)S(1)} %get-tuple-element.21), channel_id=1, source_target_pairs={{0,1},{1,2},{2,3},{3,4},{4,5},{5,6},{6,7},{7,8},{8,9},{9,10},{10,1... | collective-permute-start | bytes 737288 | tf_op jit(solution)/shard_map/ppermute | solution.py:14
  298.9 15.1 %collective-permute-start.15 = (f32[5,24,512]{2,1,0:T(8,128)S(1)}, f32[5,24,512]{2,1,0:T(8,128)S(1)}, u32[]{:S(2)}, u32[]{:S(2)}) collective-permute-start(f32[5,24,512]{2,1,0:T(8,128)S(1)} %get-tuple-element.22), channel_id=1, source_target_pairs={{1,0},{2,1},{3,2},{4,3},{5,4},{6,5},{7,6},{8,7},{9,8},{10,9},{11,1... | collective-permute-start | bytes 737288 | tf_op jit(solution)/shard_map/ppermute | solution.py:17
  354.7 60.1 %copy-start.2 = (f32[8,16,768]{2,1,0:T(8,128)S(1)}, f32[8,16,768]{2,1,0:T(8,128)}, u32[]{:S(2)}) copy-start(f32[8,16,768]{2,1,0:T(8,128)} %param.5) | copy-start | bytes 1179652
  362.8 9.1 %collective-permute-start.16 = (f32[8,15,768]{2,1,0:T(8,128)S(1)}, f32[8,15,768]{2,1,0:T(8,128)S(1)}, u32[]{:S(2)}, u32[]{:S(2)}) collective-permute-start(f32[8,15,768]{2,1,0:T(8,128)S(1)} %get-tuple-element.19), channel_id=1, source_target_pairs={{0,16},{16,32},{32,48},{48,64},{64,80},{80,96},{96,112},{112,128},... | collective-permute-start | bytes 1105928 | tf_op jit(solution)/shard_map/ppermute | solution.py:14
  364.7 9.5 %collective-permute-start.17 = (f32[8,15,768]{2,1,0:T(8,128)S(1)}, f32[8,15,768]{2,1,0:T(8,128)S(1)}, u32[]{:S(2)}, u32[]{:S(2)}) collective-permute-start(f32[8,15,768]{2,1,0:T(8,128)S(1)} %get-tuple-element.20), channel_id=1, source_target_pairs={{16,0},{32,16},{48,32},{64,48},{80,64},{96,80},{112,96},{128,112},... | collective-permute-start | bytes 1105928 | tf_op jit(solution)/shard_map/ppermute | solution.py:17
  395.9 13.4 %collective-permute-start.18 = (f32[5,16,768]{2,1,0:T(8,128)S(1)}, f32[5,16,768]{2,1,0:T(8,128)S(1)}, u32[]{:S(2)}, u32[]{:S(2)}) collective-permute-start(f32[5,16,768]{2,1,0:T(8,128)S(1)} %get-tuple-element.17), channel_id=1, source_target_pairs={{0,1},{1,2},{2,3},{3,4},{4,5},{5,6},{6,7},{7,8},{8,9},{9,10},{10,1... | collective-permute-start | bytes 737288 | tf_op jit(solution)/shard_map/ppermute | solution.py:14
  399.0 15.7 %collective-permute-start.19 = (f32[5,16,768]{2,1,0:T(8,128)S(1)}, f32[5,16,768]{2,1,0:T(8,128)S(1)}, u32[]{:S(2)}, u32[]{:S(2)}) collective-permute-start(f32[5,16,768]{2,1,0:T(8,128)S(1)} %get-tuple-element.18), channel_id=1, source_target_pairs={{1,0},{2,1},{3,2},{4,3},{5,4},{6,5},{7,6},{8,7},{9,8},{10,9},{11,1... | collective-permute-start | bytes 737288 | tf_op jit(solution)/shard_map/ppermute | solution.py:17
  429.9 9.1 %collective-permute-start.20 = (f32[8,15,768]{2,1,0:T(8,128)S(1)}, f32[8,15,768]{2,1,0:T(8,128)S(1)}, u32[]{:S(2)}, u32[]{:S(2)}) collective-permute-start(f32[8,15,768]{2,1,0:T(8,128)S(1)} %get-tuple-element.15), channel_id=1, source_target_pairs={{0,16},{16,32},{32,48},{48,64},{64,80},{80,96},{96,112},{112,128},... | collective-permute-start | bytes 1105928 | tf_op jit(solution)/shard_map/ppermute | solution.py:14
  431.9 12.7 %collective-permute-start.21 = (f32[8,15,768]{2,1,0:T(8,128)S(1)}, f32[8,15,768]{2,1,0:T(8,128)S(1)}, u32[]{:S(2)}, u32[]{:S(2)}) collective-permute-start(f32[8,15,768]{2,1,0:T(8,128)S(1)} %get-tuple-element.16), channel_id=1, source_target_pairs={{16,0},{32,16},{48,32},{64,48},{80,64},{96,80},{112,96},{128,112},... | collective-permute-start | bytes 1105928 | tf_op jit(solution)/shard_map/ppermute | solution.py:17
  466.3 13.7 %collective-permute-start.22 = (f32[5,16,768]{2,1,0:T(8,128)S(1)}, f32[5,16,768]{2,1,0:T(8,128)S(1)}, u32[]{:S(2)}, u32[]{:S(2)}) collective-permute-start(f32[5,16,768]{2,1,0:T(8,128)S(1)} %get-tuple-element.13), channel_id=1, source_target_pairs={{0,1},{1,2},{2,3},{3,4},{4,5},{5,6},{6,7},{7,8},{8,9},{9,10},{10,1... | collective-permute-start | bytes 737288 | tf_op jit(solution)/shard_map/ppermute | solution.py:14
  468.5 15.3 %collective-permute-start.23 = (f32[5,16,768]{2,1,0:T(8,128)S(1)}, f32[5,16,768]{2,1,0:T(8,128)S(1)}, u32[]{:S(2)}, u32[]{:S(2)}) collective-permute-start(f32[5,16,768]{2,1,0:T(8,128)S(1)} %get-tuple-element.14), channel_id=1, source_target_pairs={{1,0},{2,1},{3,2},{4,3},{5,4},{6,5},{7,6},{8,7},{9,8},{10,9},{11,1... | collective-permute-start | bytes 737288 | tf_op jit(solution)/shard_map/ppermute | solution.py:17
  526.2 60.9 %copy-start.4 = (f32[8,24,512]{2,1,0:T(8,128)S(1)}, f32[8,24,512]{2,1,0:T(8,128)}, u32[]{:S(2)}) copy-start(f32[8,24,512]{2,1,0:T(8,128)} %param.6) | copy-start | bytes 1179652
  537.9 7.7 %collective-permute-start.24 = (f32[8,15,512]{2,1,0:T(8,128)S(1)}, f32[8,15,512]{2,1,0:T(8,128)S(1)}, u32[]{:S(2)}, u32[]{:S(2)}) collective-permute-start(f32[8,15,512]{2,1,0:T(8,128)S(1)} %get-tuple-element.11), channel_id=1, source_target_pairs={{0,16},{16,32},{32,48},{48,64},{64,80},{80,96},{96,112},{112,128},... | collective-permute-start | bytes 737288 | tf_op jit(solution)/shard_map/ppermute | solution.py:14
  539.8 7.5 %collective-permute-start.25 = (f32[8,15,512]{2,1,0:T(8,128)S(1)}, f32[8,15,512]{2,1,0:T(8,128)S(1)}, u32[]{:S(2)}, u32[]{:S(2)}) collective-permute-start(f32[8,15,512]{2,1,0:T(8,128)S(1)} %get-tuple-element.12), channel_id=1, source_target_pairs={{16,0},{32,16},{48,32},{64,48},{80,64},{96,80},{112,96},{128,112},... | collective-permute-start | bytes 737288 | tf_op jit(solution)/shard_map/ppermute | solution.py:17
  568.7 13.4 %collective-permute-start.26 = (f32[5,24,512]{2,1,0:T(8,128)S(1)}, f32[5,24,512]{2,1,0:T(8,128)S(1)}, u32[]{:S(2)}, u32[]{:S(2)}) collective-permute-start(f32[5,24,512]{2,1,0:T(8,128)S(1)} %get-tuple-element.9), channel_id=1, source_target_pairs={{0,1},{1,2},{2,3},{3,4},{4,5},{5,6},{6,7},{7,8},{8,9},{9,10},{10,1... | collective-permute-start | bytes 737288 | tf_op jit(solution)/shard_map/ppermute | solution.py:14
  571.6 15.5 %collective-permute-start.27 = (f32[5,24,512]{2,1,0:T(8,128)S(1)}, f32[5,24,512]{2,1,0:T(8,128)S(1)}, u32[]{:S(2)}, u32[]{:S(2)}) collective-permute-start(f32[5,24,512]{2,1,0:T(8,128)S(1)} %get-tuple-element.10), channel_id=1, source_target_pairs={{1,0},{2,1},{3,2},{4,3},{5,4},{6,5},{7,6},{8,7},{9,8},{10,9},{11,1... | collective-permute-start | bytes 737288 | tf_op jit(solution)/shard_map/ppermute | solution.py:17
  602.1 7.7 %collective-permute-start.28 = (f32[8,15,512]{2,1,0:T(8,128)S(1)}, f32[8,15,512]{2,1,0:T(8,128)S(1)}, u32[]{:S(2)}, u32[]{:S(2)}) collective-permute-start(f32[8,15,512]{2,1,0:T(8,128)S(1)} %get-tuple-element.7), channel_id=1, source_target_pairs={{0,16},{16,32},{32,48},{48,64},{64,80},{80,96},{96,112},{112,128},... | collective-permute-start | bytes 737288 | tf_op jit(solution)/shard_map/ppermute | solution.py:14
  604.3 9.9 %collective-permute-start.29 = (f32[8,15,512]{2,1,0:T(8,128)S(1)}, f32[8,15,512]{2,1,0:T(8,128)S(1)}, u32[]{:S(2)}, u32[]{:S(2)}) collective-permute-start(f32[8,15,512]{2,1,0:T(8,128)S(1)} %get-tuple-element.8), channel_id=1, source_target_pairs={{16,0},{32,16},{48,32},{64,48},{80,64},{96,80},{112,96},{128,112},... | collective-permute-start | bytes 737288 | tf_op jit(solution)/shard_map/ppermute | solution.py:17
  635.6 12.2 %collective-permute-start.30 = (f32[5,24,512]{2,1,0:T(8,128)S(1)}, f32[5,24,512]{2,1,0:T(8,128)S(1)}, u32[]{:S(2)}, u32[]{:S(2)}) collective-permute-start(f32[5,24,512]{2,1,0:T(8,128)S(1)} %get-tuple-element.5), channel_id=1, source_target_pairs={{0,1},{1,2},{2,3},{3,4},{4,5},{5,6},{6,7},{7,8},{8,9},{9,10},{10,1... | collective-permute-start | bytes 737288 | tf_op jit(solution)/shard_map/ppermute | solution.py:14
  638.2 15.0 %collective-permute-start.31 = (f32[5,24,512]{2,1,0:T(8,128)S(1)}, f32[5,24,512]{2,1,0:T(8,128)S(1)}, u32[]{:S(2)}, u32[]{:S(2)}) collective-permute-start(f32[5,24,512]{2,1,0:T(8,128)S(1)} %get-tuple-element.6), channel_id=1, source_target_pairs={{1,0},{2,1},{3,2},{4,3},{5,4},{6,5},{7,6},{8,7},{9,8},{10,9},{11,1... | collective-permute-start | bytes 737288 | tf_op jit(solution)/shard_map/ppermute | solution.py:17
where the time goes:
time: 706 us; the launch traced here: 695 us
  other arithmetic  307 us (43%)
  waiting for transfers between devices  148 us (21%)
  starting transfers between devices  119 us (17%)
  blocking collectives  69.6 us (10%)
  local copies, waits for them, and re-layouts  49.4 us (7%)
    add x18, other arithmetic, weigh(): summed + weights[offset] * lax.slice_in_dim(padded, offset, offset + exte...  253 us
    ppermute x16, waiting for transfers between devices, padded_2(): lax.ppermute(lax.slice_in_dim(block, block.shape[dim] - width, None, axis...  70.2 us
    all_to_all x3, blocking collectives, reframe(): lax.all_to_all(volume, 'row', split_axis=2, concat_axis=1, tiled=True)  69.6 us
    ppermute x16, waiting for transfers between devices, padded_2(): lax.ppermute(lax.slice_in_dim(block, 0, width, axis=dim), axis, backward)  64.1 us
    ppermute x16, starting transfers between devices, padded_2(): lax.ppermute(lax.slice_in_dim(block, 0, width, axis=dim), axis, backward)  59.6 us
    ppermute x16, starting transfers between devices, padded_2(): lax.ppermute(lax.slice_in_dim(block, block.shape[dim] - width, None, axis...  40.7 us
    all_to_all x9, local copies, waits for them, and re-layouts, reframe(): lax.all_to_all(volume, 'row', split_axis=2, concat_axis=1, tiled=True)  25.5 us
    all_to_all x1, starting transfers between devices, reframe(): lax.all_to_all(volume, 'row', split_axis=2, concat_axis=1, tiled=True)  18.7 us
  transfers between devices with their start and end apart: 33, of which 32 were waited for; matrix products, arithmetic and copies ran while one was open for 1% of the time, Pallas kernels for 0%

commit v1 on v0

v1 whole, which is shorter than its diff:
```python
import functools
import jax
import jax.numpy as jnp
from jax import lax
from jax.experimental import pallas as pl
from jax.experimental.pallas import tpu as pltpu
from jax.sharding import PartitionSpec as P

ITERS = 2
LANES = 128
SHIFT = 64
HIGH = lax.Precision.HIGHEST
VMEM = pl.BlockSpec(memory_space=pltpu.VMEM)
SMEM = pl.BlockSpec(memory_space=pltpu.SMEM)


def splat(value):
    return jnp.full((8, LANES), value, jnp.float32)


def prepare_body(axial_ref, lateral_ref, ya_ref, yb_ref, za_ref, zb_ref, band_ref):
    axial, lateral = axial_ref.shape[1], lateral_ref.shape[2]

    def normalized(read, count):
        taps = [read(k) for k in range(count)]
        total = taps[0]
        for tap in taps[1:]:
            total = total + tap
        total = splat(total)
        return [splat(tap) / total for tap in taps]

    rows = (
        (ya_ref, lambda k: axial_ref[0, k], axial),
        (yb_ref, lambda k: lateral_ref[1, 1, k], lateral),
        (za_ref, lambda k: lateral_ref[0, 0, k], lateral),
        (zb_ref, lambda k: lateral_ref[1, 0, k], lateral),
    )
    for target, read, count in rows:
        for k, tap in enumerate(normalized(read, count)):
            target[k] = tap
    xa = normalized(lambda k: lateral_ref[0, 1, k], lateral)
    xb = normalized(lambda k: axial_ref[1, k], axial)
    lane = lax.broadcasted_iota(jnp.int32, (8, LANES), 1)
    sub = lax.broadcasted_iota(jnp.int32, (8, LANES), 0)

    def fill(step, carry):
        distance = sub + step * 8 - lane - SHIFT
        for index, taps in enumerate((xa, xb)):
            half = len(taps) // 2
            ahead = jnp.zeros((8, LANES), jnp.float32)
            back = jnp.zeros((8, LANES), jnp.float32)
            for k, tap in enumerate(taps):
                ahead = jnp.where(distance == k - half, tap, ahead)
                back = jnp.where(distance == half - k, tap, back)
            at = pl.ds(pl.multiple_of(step * 8, 8), 8)
            band_ref[2 * index, at, :] = ahead
            band_ref[2 * index + 1, at, :] = back
        return carry

    lax.fori_loop(0, 2 * LANES // 8, fill, 0)


def prepare(axial_kernel, lateral_kernel):
    axial, lateral = axial_kernel.shape[1], lateral_kernel.shape[2]
    shapes = [(axial, 8, LANES), (lateral, 8, LANES), (lateral, 8, LANES), (lateral, 8, LANES)]
    shapes.append((4, 2 * LANES, LANES))
    return pl.pallas_call(
        prepare_body,
        out_shape=[jax.ShapeDtypeStruct(shape, jnp.float32) for shape in shapes],
        in_specs=[SMEM, SMEM],
        out_specs=[VMEM] * 5,
        name="prepare",
    )(axial_kernel, lateral_kernel)


def correlate(taps, rows, extent, reverse):
    count = len(taps)
    sums = [None] * extent
    for r in range(extent + count - 1):
        value = rows(r)
        for i in range(max(0, r - count + 1), min(extent, r + 1)):
            k = r - i
            term = taps[count - 1 - k if reverse else k] * value
            sums[i] = term if sums[i] is None else sums[i] + term
    return sums


def padded_rows(low, mid, high, pick):
    margin, extent = low.shape[0], mid.shape[0]

    def rows(r):
        if r < margin:
            return pick(low, r)
        if r < margin + extent:
            return pick(mid, r - margin)
        return pick(high, r - margin - extent)

    return rows


def lanes_at(j):
    return pl.ds(pl.multiple_of(j * LANES, LANES), LANES)


def along_z(taps_ref, low_ref, mid_ref, high_ref, reverse, store):
    rows_y, width = mid_ref.shape[1], mid_ref.shape[2]

    def tile(j, carry):
        lanes = lanes_at(j)
        taps = [taps_ref[k] for k in range(taps_ref.shape[0])]
        for y in range(0, rows_y, 8):
            pick = lambda ref, r: ref[r, y:y + 8, lanes]
            sums = correlate(taps, padded_rows(low_ref, mid_ref, high_ref, pick), mid_ref.shape[0], reverse)
            store(y, j, sums)
        return carry

    lax.fori_loop(0, width // LANES, tile, 0)


def depth_body(reverse, taps_ref, low_ref, mid_ref, high_ref, out_ref):
    def store(y, j, sums):
        out_ref[y:y + 8, :, lanes_at(j)] = jnp.swapaxes(jnp.stack(sums), 0, 1)

    along_z(taps_ref, low_ref, mid_ref, high_ref, reverse, store)


def depth(taps, low, mid, high, reverse):
    nz, ny, nx = mid.shape
    return pl.pallas_call(
        functools.partial(depth_body, reverse),
        out_shape=jax.ShapeDtypeStruct((ny, nz, nx), jnp.float32),
        in_specs=[VMEM] * 4,
        out_specs=VMEM,
        name="depth",
    )(taps, low, mid, high)


def plane_body(reverse, divide, taps_ref, low_ref, mid_ref, high_ref, *refs):
    view_ref, out_ref = refs if divide else (None, refs[0])

    def tile(j, carry):
        lanes = lanes_at(j)
        taps = [taps_ref[k] for k in range(taps_ref.shape[0])]
        pick = lambda ref, r: ref[r, :, lanes]
        sums = correlate(taps, padded_rows(low_ref, mid_ref, high_ref, pick), mid_ref.shape[0], reverse)
        if divide:
            for i, value in enumerate(sums):
                out_ref[i, :, lanes] = view_ref[i, :, lanes] / value
        else:
            for y in range(0, len(sums), 8):
                out_ref[:, y:y + 8, lanes] = jnp.swapaxes(jnp.stack(sums[y:y + 8]), 0, 1)
        return carry

    lax.fori_loop(0, mid_ref.shape[2] // LANES, tile, 0)


def plane(taps, low, mid, high, reverse, view=None):
    ny, nz, nx = mid.shape
    shape = (nz, ny, nx) if view is None else (ny, nz, nx)
    operands = (taps, low, mid, high) + (() if view is None else (view,))
    return pl.pallas_call(
        functools.partial(plane_body, reverse, view is not None),
        out_shape=jax.ShapeDtypeStruct(shape, jnp.float32),
        in_specs=[VMEM] * len(operands),
        out_specs=VMEM,
        name="plane",
    )(*operands)


def clear_edges(wide_ref):
    blank = jnp.zeros((wide_ref.shape[0], LANES), jnp.float32)
    wide_ref[:, :LANES] = blank
    wide_ref[:, wide_ref.shape[1] - LANES:] = blank


def along_x(wide_ref, band):
    width = wide_ref.shape[1] - LANES
    for j in range(width // LANES):
        yield j, jnp.dot(
            wide_ref[:, j * LANES:(j + 2) * LANES], band, precision=HIGH, preferred_element_type=jnp.float32
        )


def first_body(band_ref, estimate_ref, out_ref, wide_ref):
    nz, ny, nx = estimate_ref.shape
    clear_edges(wide_ref)
    wide_ref[:, SHIFT:SHIFT + nx] = estimate_ref[...].reshape(nz * ny, nx)
    for j, value in along_x(wide_ref, band_ref[...]):
        out_ref[:, :, j * LANES:(j + 1) * LANES] = value.reshape(nz, ny, LANES)


def first(band, estimate):
    nz, ny, nx = estimate.shape
    return pl.pallas_call(
        first_body,
        out_shape=jax.ShapeDtypeStruct(estimate.shape, jnp.float32),
        in_specs=[VMEM] * 2,
        out_specs=VMEM,
        scratch_shapes=[pltpu.VMEM((nz * ny, nx + LANES), jnp.float32)],
        name="first",
    )(band, estimate)


def update_body(last, taps_ref, low_ref, mid_ref, high_ref, band_ref, estimate_ref, *refs):
    if last:
        out_ref, wide_ref, mixed_ref = refs
    else:
        next_ref, out_ref, ahead_ref, wide_ref, mixed_ref = refs
    nz, ny, nx = mid_ref.shape

    def store(y, j, sums):
        for z, value in enumerate(sums):
            mixed_ref[z * ny + y:z * ny + y + 8, lanes_at(j)] = value

    along_z(taps_ref, low_ref, mid_ref, high_ref, True, store)
    clear_edges(wide_ref)
    wide_ref[:, SHIFT:SHIFT + nx] = mixed_ref[...]
    for j, value in along_x(wide_ref, band_ref[...]):
        at = slice(j * LANES, (j + 1) * LANES)
        out_ref[:, :, at] = estimate_ref[:, :, at] * value.reshape(nz, ny, LANES)
    if not last:
        wide_ref[:, SHIFT:SHIFT + nx] = out_ref[...].reshape(nz * ny, nx)
        for j, value in along_x(wide_ref, next_ref[...]):
            ahead_ref[:, :, j * LANES:(j + 1) * LANES] = value.reshape(nz, ny, LANES)


def update(taps, low, mid, high, band, estimate, band_next=None):
    nz, ny, nx = mid.shape
    last = band_next is None
    operands = (taps, low, mid, high, band, estimate) + (() if last else (band_next,))
    shape = jax.ShapeDtypeStruct(mid.shape, jnp.float32)
    return pl.pallas_call(
        functools.partial(update_body, last),
        out_shape=[shape] if last else [shape, shape],
        in_specs=[VMEM] * len(operands),
        out_specs=[VMEM] * (1 if last else 2),
        scratch_shapes=[
            pltpu.VMEM((nz * ny, nx + LANES), jnp.float32),
            pltpu.VMEM((nz * ny, nx), jnp.float32),
        ],
        name="update",
    )(*operands)


def exchange(block, axis, width):
    count = lax.axis_size(axis)
    forward = [(i, i + 1) for i in range(count - 1)]
    backward = [(target, source) for source, target in forward]
    extent = block.shape[0]
    low = lax.ppermute(lax.slice_in_dim(block, extent - width, extent, axis=0), axis, forward)
    high = lax.ppermute(lax.slice_in_dim(block, 0, width, axis=0), axis, backward)
    return low, block, high


def reframe(view):
    nz, nx, ny = view.shape
    count = lax.axis_size("row")
    rows = ny // count
    pieces = view.reshape(nz, nx, count, rows).transpose(2, 1, 3, 0).reshape(count, nx, rows * nz)
    arrived = lax.all_to_all(pieces, "row", 0, 0, tiled=True)
    return arrived.reshape(count * nx, rows * nz).T.reshape(rows, nz, count * nx)


def per_device(view_a, view_b, estimate, axial_kernel, lateral_kernel):
    ya, yb, za, zb, bands = prepare(axial_kernel, lateral_kernel)
    views = (jnp.swapaxes(view_a, 0, 1), reframe(view_b))
    ytaps, ztaps = (ya, yb), (za, zb)
    ahead = first(bands[0], estimate)
    steps = 2 * ITERS
    for step in range(steps):
        v = step % 2
        yt, zt, view = ytaps[v], ztaps[v], views[v]
        margin = yt.shape[0] // 2
        blurred = depth(zt, *exchange(ahead, "col", zt.shape[0] // 2), False)
        quotient = plane(yt, *exchange(blurred, "row", margin), False, view)
        spread = plane(yt, *exchange(quotient, "row", margin), True)
        halo = exchange(spread, "col", zt.shape[0] // 2)
        if step == steps - 1:
            (estimate,) = update(zt, *halo, bands[2 * v + 1], estimate)
        else:
            estimate, ahead = update(zt, *halo, bands[2 * v + 1], estimate, bands[2 * (1 - v)])
    return estimate


def solution(mesh):
    in_specs = (P("col", "row", None), P("col", "row", None), P("col", "row", None), P(), P())
    out_specs = P("col", "row", None)
    return jax.shard_map(
        per_device, mesh=mesh, in_specs=in_specs, out_specs=out_specs, check_vma=False
    )
```

time: 706 us -> 332 us (0.47)
  the two profiles are of different devices: /device:TPU:58 before, /device:TPU:68 now
where the time goes in v1:
time: 332 us; the launch traced here: 330 us
  waiting for transfers between devices  132 us (40%)
  starting transfers between devices  108 us (33%)
  Pallas kernels  51.5 us (16%)
  local copies, waits for them, and re-layouts  38.1 us (11%)
    ppermute x16, waiting for transfers between devices, exchange(): lax.ppermute(lax.slice_in_dim(block, extent - width, extent, axis=0), axi...  75.7 us
    ppermute x16, waiting for transfers between devices, exchange(): lax.ppermute(lax.slice_in_dim(block, 0, width, axis=0), axis, backward)  55.9 us
    ppermute x16, starting transfers between devices, exchange(): lax.ppermute(lax.slice_in_dim(block, extent - width, extent, axis=0), axi...  50.3 us
    ppermute x16, starting transfers between devices, exchange(): lax.ppermute(lax.slice_in_dim(block, 0, width, axis=0), axis, backward)  45.7 us
    pallas_call x8, Pallas kernels, plane(): pl.pallas_call(functools.partial(plane_body, reverse, view is not None),...  21.5 us
    slice x16, local copies, waits for them, and re-layouts, exchange(): lax.slice_in_dim(block, 0, width, axis=0)  18.1 us
    pallas_call x4, Pallas kernels, update(): pl.pallas_call(functools.partial(update_body, last), out_shape=[shape] if...  15.2 us
    all_to_all x1, starting transfers between devices, reframe(): arrived = lax.all_to_all(pieces, 'row', 0, 0, tiled=True)  12.5 us
  transfers between devices with their start and end apart: 33, of which 26 were waited for; matrix products, arithmetic and copies ran while one was open for 3% of the time, Pallas kernels for 2%

profile of v1, /device:TPU:68, one launch (start us, length us, event | category | flops | bytes accessed | tf_op | source)
XLA Modules:
  0.0 330.1 jit_solution(7362330369988072266)
XLA Ops:
  0.0 2.8 prepare.1
  4.7 2.6 first.1.mid_ref
  8.4 6.1 %collective-permute-start.1 = (f32[5,16,768]{2,1,0:T(8,128)S(1)}, f32[5,16,768]{2,1,0:T(8,128)S(1)}, u32[]{:S(2)}, u32[]{:S(2)}) collective-permute-start(f32[5,16,768]{2,1,0:T(8,128)S(1)} %get-tuple-element.61), channel_id=1, source_target_pairs={{1,0},{2,1},{3,2},{4,3},{5,4},{6,5},{7,6},{8,7},{9,8},{10,9},{11,1... | collective-permute-start | bytes 737288 | tf_op jit(solution)/shard_map/ppermute | solution.py:251
  16.5 8.6 %collective-permute-done.1.high_ref = f32[5,16,768]{2,1,0:T(8,128)S(1)} collective-permute-done((f32[5,16,768]{2,1,0:T(8,128)S(1)}, f32[5,16,768]{2,1,0:T(8,128)S(1)}, u32[]{:S(2)}, u32[]{:S(2)}) %collective-permute-start.1) | collective-permute-done | bytes 245792 | tf_op jit(solution)/shard_map/ppermute | solution.py:251
  25.0 6.3 %collective-permute-done.low_ref = f32[5,16,768]{2,1,0:T(8,128)S(1)} collective-permute-done((f32[5,16,768]{2,1,0:T(8,128)S(1)}, f32[5,16,768]{2,1,0:T(8,128)S(1)}, u32[]{:S(2)}, u32[]{:S(2)}) %collective-permute-start) | collective-permute-done | bytes 245792 | tf_op jit(solution)/shard_map/ppermute | solution.py:250
  32.1 2.3 depth.4.mid_ref
  37.5 2.4 collective-permute-start.2
  40.9 3.1 collective-permute-done.3.high_ref
  44.0 3.3 collective-permute-done.2.low_ref
  47.9 3.2 plane.8.mid_ref
  54.2 2.4 collective-permute-start.4
  56.6 3.5 %collective-permute-done.5.high_ref = f32[15,8,768]{2,1,0:T(8,128)S(1)} collective-permute-done((f32[15,8,768]{2,1,0:T(8,128)S(1)}, f32[15,8,768]{2,1,0:T(8,128)S(1)}, u32[]{:S(2)}, u32[]{:S(2)}) %collective-permute-start.5) | collective-permute-done | bytes 368672 | tf_op jit(solution)/shard_map/ppermute | solution.py:251
  60.1 3.8 %collective-permute-done.4.low_ref = f32[15,8,768]{2,1,0:T(8,128)S(1)} collective-permute-done((f32[15,8,768]{2,1,0:T(8,128)S(1)}, f32[15,8,768]{2,1,0:T(8,128)S(1)}, u32[]{:S(2)}, u32[]{:S(2)}) %collective-permute-start.4) | collective-permute-done | bytes 368672 | tf_op jit(solution)/shard_map/ppermute | solution.py:250
  64.6 2.9 plane.9.mid_ref
  69.5 2.3 collective-permute-start.7
  71.7 4.5 %collective-permute-start.6 = (f32[5,16,768]{2,1,0:T(8,128)}, f32[5,16,768]{2,1,0:T(8,128)}, u32[]{:S(2)}, u32[]{:S(2)}) collective-permute-start(f32[5,16,768]{2,1,0:T(8,128)} %get-tuple-element.56), channel_id=1, source_target_pairs={{0,1},{1,2},{2,3},{3,4},{4,5},{5,6},{6,7},{7,8},{8,9},{9,10},{10,1... | collective-permute-start | bytes 737288 | tf_op jit(solution)/shard_map/ppermute | solution.py:250
  79.3 2.6 copy.13
  81.9 12.5 %all-to-all-start = ((f32[32,24,128]{2,1,0:T(8,128)}), f32[32,24,128]{2,1,0:T(8,128)S(1)}, u32[]{:S(2)}, u32[]{:S(2)}) async-start(f32[32,24,128]{2,1,0:T(8,128)} %copy.13), calls=%async_computation | async-start | bytes 786432 | tf_op jit(solution)/shard_map/all_to_all | solution.py:260
  94.5 4.0 %update.4 = (f32[8,16,768]{2,1,0:T(8,128)}, f32[8,16,768]{2,1,0:T(8,128)}) custom-call(f32[11,8,128]{2,1,0:T(8,128)} %get-tuple-element.18.taps_ref, f32[5,16,768]{2,1,0:T(8,128)} %collective-permute-done.6.low_ref, f32[8,16,768]{2,1,0:T(8,128)} %plane.9.mid_ref, f32[5,16,768]{2,1,0:T(8,128)} %collective-permute-done.7.high_ref, ...), custom_call_target="tpu_custom_call" | custom-call | tf_op jit(solution)/shard_map/update/pallas_call | solution.py:232
  99.6 4.0 %collective-permute-start.9 = (f32[5,16,768]{2,1,0:T(8,128)S(1)}, f32[5,16,768]{2,1,0:T(8,128)S(1)}, u32[]{:S(2)}, u32[]{:S(2)}) collective-permute-start(f32[5,16,768]{2,1,0:T(8,128)S(1)} %get-tuple-element.53), channel_id=1, source_target_pairs={{1,0},{2,1},{3,2},{4,3},{5,4},{6,5},{7,6},{8,7},{9,8},{10,9},{11,1... | collective-permute-start | bytes 737288 | tf_op jit(solution)/shard_map/ppermute | solution.py:251
  103.6 2.7 collective-permute-start.8
  106.3 6.6 %collective-permute-done.9.high_ref = f32[5,16,768]{2,1,0:T(8,128)S(1)} collective-permute-done((f32[5,16,768]{2,1,0:T(8,128)S(1)}, f32[5,16,768]{2,1,0:T(8,128)S(1)}, u32[]{:S(2)}, u32[]{:S(2)}) %collective-permute-start.9) | collective-permute-done | bytes 245792 | tf_op jit(solution)/shard_map/ppermute | solution.py:251
  112.9 8.6 %collective-permute-done.8.low_ref = f32[5,16,768]{2,1,0:T(8,128)S(1)} collective-permute-done((f32[5,16,768]{2,1,0:T(8,128)S(1)}, f32[5,16,768]{2,1,0:T(8,128)S(1)}, u32[]{:S(2)}, u32[]{:S(2)}) %collective-permute-start.8) | collective-permute-done | bytes 245792 | tf_op jit(solution)/shard_map/ppermute | solution.py:250
  122.2 2.3 depth.5.mid_ref
  127.4 2.4 collective-permute-start.10
  130.8 3.7 %collective-permute-done.10.low_ref = f32[5,8,768]{2,1,0:T(8,128)S(1)} collective-permute-done((f32[5,8,768]{2,1,0:T(8,128)S(1)}, f32[5,8,768]{2,1,0:T(8,128)S(1)}, u32[]{:S(2)}, u32[]{:S(2)}) %collective-permute-start.10) | collective-permute-done | bytes 122912 | tf_op jit(solution)/shard_map/ppermute | solution.py:250
  135.2 2.4 plane.10.mid_ref
  140.5 2.4 collective-permute-start.12
  142.9 4.7 %collective-permute-done.12.low_ref = f32[5,8,768]{2,1,0:T(8,128)S(1)} collective-permute-done((f32[5,8,768]{2,1,0:T(8,128)S(1)}, f32[5,8,768]{2,1,0:T(8,128)S(1)}, u32[]{:S(2)}, u32[]{:S(2)}) %collective-permute-start.12) | collective-permute-done | bytes 122912 | tf_op jit(solution)/shard_map/ppermute | solution.py:250
  153.5 4.8 %collective-permute-start.14 = (f32[5,16,768]{2,1,0:T(8,128)S(1)}, f32[5,16,768]{2,1,0:T(8,128)S(1)}, u32[]{:S(2)}, u32[]{:S(2)}) collective-permute-start(f32[5,16,768]{2,1,0:T(8,128)S(1)} %get-tuple-element.48), channel_id=1, source_target_pairs={{0,1},{1,2},{2,3},{3,4},{4,5},{5,6},{6,7},{7,8},{8,9},{9,10},{10,1... | collective-permute-start | bytes 737288 | tf_op jit(solution)/shard_map/ppermute | solution.py:250
  158.3 6.6 %collective-permute-done.15.high_ref = f32[5,16,768]{2,1,0:T(8,128)S(1)} collective-permute-done((f32[5,16,768]{2,1,0:T(8,128)S(1)}, f32[5,16,768]{2,1,0:T(8,128)S(1)}, u32[]{:S(2)}, u32[]{:S(2)}) %collective-permute-start.15) | collective-permute-done | bytes 245792 | tf_op jit(solution)/shard_map/ppermute | solution.py:251
  164.9 3.8 %collective-permute-done.14.low_ref = f32[5,16,768]{2,1,0:T(8,128)S(1)} collective-permute-done((f32[5,16,768]{2,1,0:T(8,128)S(1)}, f32[5,16,768]{2,1,0:T(8,128)S(1)}, u32[]{:S(2)}, u32[]{:S(2)}) %collective-permute-start.14) | collective-permute-done | bytes 245792 | tf_op jit(solution)/shard_map/ppermute | solution.py:250
  169.4 4.0 %update.5 = (f32[8,16,768]{2,1,0:T(8,128)}, f32[8,16,768]{2,1,0:T(8,128)}) custom-call(f32[11,8,128]{2,1,0:T(8,128)} %get-tuple-element.16.taps_ref, f32[5,16,768]{2,1,0:T(8,128)} %copy-done.14, f32[8,16,768]{2,1,0:T(8,128)} %plane.11.mid_ref, f32[5,16,768]{2,1,0:T(8,128)} %copy-done.11, f32[256,128]{1,0:T(8,128)} %get-tuple-element.27.band_ref, ...), custom_call_target="tpu_custom_call" | custom-call | tf_op jit(solution)/shard_map/update/pallas_call | solution.py:232
  176.4 4.8 %collective-permute-start.16 = (f32[5,16,768]{2,1,0:T(8,128)S(1)}, f32[5,16,768]{2,1,0:T(8,128)S(1)}, u32[]{:S(2)}, u32[]{:S(2)}) collective-permute-start(f32[5,16,768]{2,1,0:T(8,128)S(1)} %get-tuple-element.46), channel_id=1, source_target_pairs={{0,1},{1,2},{2,3},{3,4},{4,5},{5,6},{6,7},{7,8},{8,9},{9,10},{10,1... | collective-permute-start | bytes 737288 | tf_op jit(solution)/shard_map/ppermute | solution.py:250
  181.3 6.8 %collective-permute-done.17.high_ref = f32[5,16,768]{2,1,0:T(8,128)S(1)} collective-permute-done((f32[5,16,768]{2,1,0:T(8,128)S(1)}, f32[5,16,768]{2,1,0:T(8,128)S(1)}, u32[]{:S(2)}, u32[]{:S(2)}) %collective-permute-start.17) | collective-permute-done | bytes 245792 | tf_op jit(solution)/shard_map/ppermute | solution.py:251
  188.1 3.0 collective-permute-done.16.low_ref
  191.8 2.3 depth.6.mid_ref
  197.2 2.4 collective-permute-start.18
  199.6 3.2 collective-permute-done.19.high_ref
  202.8 4.1 %collective-permute-done.18.low_ref = f32[15,8,768]{2,1,0:T(8,128)S(1)} collective-permute-done((f32[15,8,768]{2,1,0:T(8,128)S(1)}, f32[15,8,768]{2,1,0:T(8,128)S(1)}, u32[]{:S(2)}, u32[]{:S(2)}) %collective-permute-start.18) | collective-permute-done | bytes 368672 | tf_op jit(solution)/shard_map/ppermute | solution.py:250
  207.7 3.1 plane.12.mid_ref
  213.9 2.4 collective-permute-start.20
  216.4 3.5 %collective-permute-done.21.high_ref = f32[15,8,768]{2,1,0:T(8,128)S(1)} collective-permute-done((f32[15,8,768]{2,1,0:T(8,128)S(1)}, f32[15,8,768]{2,1,0:T(8,128)S(1)}, u32[]{:S(2)}, u32[]{:S(2)}) %collective-permute-start.21) | collective-permute-done | bytes 368672 | tf_op jit(solution)/shard_map/ppermute | solution.py:251
  219.9 3.8 %collective-permute-done.20.low_ref = f32[15,8,768]{2,1,0:T(8,128)S(1)} collective-permute-done((f32[15,8,768]{2,1,0:T(8,128)S(1)}, f32[15,8,768]{2,1,0:T(8,128)S(1)}, u32[]{:S(2)}, u32[]{:S(2)}) %collective-permute-start.20) | collective-permute-done | bytes 368672 | tf_op jit(solution)/shard_map/ppermute | solution.py:250
  224.4 2.9 plane.13.mid_ref
  228.4 2.4 collective-permute-start.23
  230.8 7.1 %collective-permute-start.22 = (f32[5,16,768]{2,1,0:T(8,128)S(1)}, f32[5,16,768]{2,1,0:T(8,128)S(1)}, u32[]{:S(2)}, u32[]{:S(2)}) collective-permute-start(f32[5,16,768]{2,1,0:T(8,128)S(1)} %get-tuple-element.40), channel_id=1, source_target_pairs={{0,1},{1,2},{2,3},{3,4},{4,5},{5,6},{6,7},{7,8},{8,9},{9,10},{10,1... | collective-permute-start | bytes 737288 | tf_op jit(solution)/shard_map/ppermute | solution.py:250
  237.9 6.6 %collective-permute-done.23.high_ref = f32[5,16,768]{2,1,0:T(8,128)S(1)} collective-permute-done((f32[5,16,768]{2,1,0:T(8,128)S(1)}, f32[5,16,768]{2,1,0:T(8,128)S(1)}, u32[]{:S(2)}, u32[]{:S(2)}) %collective-permute-start.23) | collective-permute-done | bytes 245792 | tf_op jit(solution)/shard_map/ppermute | solution.py:251
  244.5 7.8 %collective-permute-done.22.low_ref = f32[5,16,768]{2,1,0:T(8,128)S(1)} collective-permute-done((f32[5,16,768]{2,1,0:T(8,128)S(1)}, f32[5,16,768]{2,1,0:T(8,128)S(1)}, u32[]{:S(2)}, u32[]{:S(2)}) %collective-permute-start.22) | collective-permute-done | bytes 245792 | tf_op jit(solution)/shard_map/ppermute | solution.py:250
  253.0 4.0 %update.6 = (f32[8,16,768]{2,1,0:T(8,128)}, f32[8,16,768]{2,1,0:T(8,128)}) custom-call(f32[11,8,128]{2,1,0:T(8,128)} %get-tuple-element.18.taps_ref, f32[5,16,768]{2,1,0:T(8,128)} %copy-done.13, f32[8,16,768]{2,1,0:T(8,128)} %plane.13.mid_ref, f32[5,16,768]{2,1,0:T(8,128)} %copy-done.10, f32[256,128]{1,0:T(8,128)} %get-tuple-element.29.band_ref, ...), custom_call_target="tpu_custom_call" | custom-call | tf_op jit(solution)/shard_map/update/pallas_call | solution.py:232
  258.1 3.4 %collective-permute-start.25 = (f32[5,16,768]{2,1,0:T(8,128)S(1)}, f32[5,16,768]{2,1,0:T(8,128)S(1)}, u32[]{:S(2)}, u32[]{:S(2)}) collective-permute-start(f32[5,16,768]{2,1,0:T(8,128)S(1)} %get-tuple-element.37), channel_id=1, source_target_pairs={{1,0},{2,1},{3,2},{4,3},{5,4},{6,5},{7,6},{8,7},{9,8},{10,9},{11,1... | collective-permute-start | bytes 737288 | tf_op jit(solution)/shard_map/ppermute | solution.py:251
  261.6 3.3 collective-permute-start.24
  264.9 3.1 collective-permute-done.25.high_ref
  267.9 6.8 %collective-permute-done.24.low_ref = f32[5,16,768]{2,1,0:T(8,128)S(1)} collective-permute-done((f32[5,16,768]{2,1,0:T(8,128)S(1)}, f32[5,16,768]{2,1,0:T(8,128)S(1)}, u32[]{:S(2)}, u32[]{:S(2)}) %collective-permute-start.24) | collective-permute-done | bytes 245792 | tf_op jit(solution)/shard_map/ppermute | solution.py:250
  275.5 2.3 depth.7.mid_ref
  280.7 2.4 collective-permute-start.26
  283.1 4.7 %collective-permute-done.26.low_ref = f32[5,8,768]{2,1,0:T(8,128)S(1)} collective-permute-done((f32[5,8,768]{2,1,0:T(8,128)S(1)}, f32[5,8,768]{2,1,0:T(8,128)S(1)}, u32[]{:S(2)}, u32[]{:S(2)}) %collective-permute-start.26) | collective-permute-done | bytes 122912 | tf_op jit(solution)/shard_map/ppermute | solution.py:250
  288.5 2.4 plane.14.mid_ref
  293.8 2.4 collective-permute-start.28
  296.2 4.7 %collective-permute-done.28.low_ref = f32[5,8,768]{2,1,0:T(8,128)S(1)} collective-permute-done((f32[5,8,768]{2,1,0:T(8,128)S(1)}, f32[5,8,768]{2,1,0:T(8,128)S(1)}, u32[]{:S(2)}, u32[]{:S(2)}) %collective-permute-start.28) | collective-permute-done | bytes 122912 | tf_op jit(solution)/shard_map/ppermute | solution.py:250
  304.9 8.3 %collective-permute-start.31 = (f32[5,16,768]{2,1,0:T(8,128)S(1)}, f32[5,16,768]{2,1,0:T(8,128)S(1)}, u32[]{:S(2)}, u32[]{:S(2)}) collective-permute-start(f32[5,16,768]{2,1,0:T(8,128)S(1)} %get-tuple-element.31), channel_id=1, source_target_pairs={{1,0},{2,1},{3,2},{4,3},{5,4},{6,5},{7,6},{8,7},{9,8},{10,9},{11,1... | collective-permute-start | bytes 737288 | tf_op jit(solution)/shard_map/ppermute | solution.py:251
  315.1 4.3 %collective-permute-done.31.high_ref = f32[5,16,768]{2,1,0:T(8,128)S(1)} collective-permute-done((f32[5,16,768]{2,1,0:T(8,128)S(1)}, f32[5,16,768]{2,1,0:T(8,128)S(1)}, u32[]{:S(2)}, u32[]{:S(2)}) %collective-permute-start.31) | collective-permute-done | bytes 245792 | tf_op jit(solution)/shard_map/ppermute | solution.py:251
  319.4 6.7 %collective-permute-done.30.low_ref = f32[5,16,768]{2,1,0:T(8,128)S(1)} collective-permute-done((f32[5,16,768]{2,1,0:T(8,128)S(1)}, f32[5,16,768]{2,1,0:T(8,128)S(1)}, u32[]{:S(2)}, u32[]{:S(2)}) %collective-permute-start.30) | collective-permute-done | bytes 245792 | tf_op jit(solution)/shard_map/ppermute | solution.py:250
  326.8 3.3 %update.7 = f32[8,16,768]{2,1,0:T(8,128)} custom-call(f32[11,8,128]{2,1,0:T(8,128)} %get-tuple-element.16.taps_ref, f32[5,16,768]{2,1,0:T(8,128)} %copy-done.19, f32[8,16,768]{2,1,0:T(8,128)} %plane.15.mid_ref, f32[5,16,768]{2,1,0:T(8,128)} %copy-done.12, f32[256,128]{1,0:T(8,128)} %get-tuple-element.27.band_ref, f32[8,16,768]{2,1,0:T(8,128)} %get-tuple-element.26.estimate_ref), custom_call_target="tpu_custom_call" | custom-call | tf_op jit(solution)/shard_map/update/pallas_call | solution.py:232
  (106 shorter events, 63.1 us)
Async XLA Ops:
  0.0 39.9 %copy-start.1 = (f32[8,16,768]{2,1,0:T(8,128)S(1)}, f32[8,16,768]{2,1,0:T(8,128)}, u32[]{:S(2)}) copy-start(f32[8,16,768]{2,1,0:T(8,128)} %param.5) | copy-start | bytes 1179652
  8.4 16.6 %collective-permute-start.1 = (f32[5,16,768]{2,1,0:T(8,128)S(1)}, f32[5,16,768]{2,1,0:T(8,128)S(1)}, u32[]{:S(2)}, u32[]{:S(2)}) collective-permute-start(f32[5,16,768]{2,1,0:T(8,128)S(1)} %get-tuple-element.61), channel_id=1, source_target_pairs={{1,0},{2,1},{3,2},{4,3},{5,4},{6,5},{7,6},{8,7},{9,8},{10,9},{11,1... | collective-permute-start | bytes 737288 | tf_op jit(solution)/shard_map/ppermute | solution.py:251
  14.6 16.8 %collective-permute-start = (f32[5,16,768]{2,1,0:T(8,128)S(1)}, f32[5,16,768]{2,1,0:T(8,128)S(1)}, u32[]{:S(2)}, u32[]{:S(2)}) collective-permute-start(f32[5,16,768]{2,1,0:T(8,128)S(1)} %get-tuple-element.62), channel_id=1, source_target_pairs={{0,1},{1,2},{2,3},{3,4},{4,5},{5,6},{6,7},{7,8},{8,9},{9,10},{10,1... | collective-permute-start | bytes 737288 | tf_op jit(solution)/shard_map/ppermute | solution.py:250
  25.0 6.3 %copy-start.15 = (f32[5,16,768]{2,1,0:T(8,128)}, f32[5,16,768]{2,1,0:T(8,128)S(1)}, u32[]{:S(2)}) copy-start(f32[5,16,768]{2,1,0:T(8,128)S(1)} %collective-permute-done.1.high_ref) | copy-start | bytes 737284
  31.4 0.7 copy-start.20
  35.5 8.4 %collective-permute-start.3 = (f32[15,8,768]{2,1,0:T(8,128)S(1)}, f32[15,8,768]{2,1,0:T(8,128)S(1)}, u32[]{:S(2)}, u32[]{:S(2)}) collective-permute-start(f32[15,8,768]{2,1,0:T(8,128)S(1)} %get-tuple-element.59), channel_id=1, source_target_pairs={{16,0},{32,16},{48,32},{64,48},{80,64},{96,80},{112,96},{128,112},... | collective-permute-start | bytes 1105928 | tf_op jit(solution)/shard_map/ppermute | solution.py:251
  37.5 9.7 %collective-permute-start.2 = (f32[15,8,768]{2,1,0:T(8,128)S(1)}, f32[15,8,768]{2,1,0:T(8,128)S(1)}, u32[]{:S(2)}, u32[]{:S(2)}) collective-permute-start(f32[15,8,768]{2,1,0:T(8,128)S(1)} %get-tuple-element.60), channel_id=1, source_target_pairs={{0,16},{16,32},{32,48},{48,64},{64,80},{80,96},{96,112},{112,128},... | collective-permute-start | bytes 1105928 | tf_op jit(solution)/shard_map/ppermute | solution.py:250
  40.9 35.3 %copy-start = (f32[8,24,512]{2,1,0:T(8,128)S(1)}, f32[8,24,512]{2,1,0:T(8,128)}, u32[]{:S(2)}) copy-start(f32[8,24,512]{2,1,0:T(8,128)} %param.6) | copy-start | bytes 1179652
  43.9 3.3 copy-start.2
  47.2 0.7 copy-start.6
  52.3 7.8 %collective-permute-start.5 = (f32[15,8,768]{2,1,0:T(8,128)S(1)}, f32[15,8,768]{2,1,0:T(8,128)S(1)}, u32[]{:S(2)}, u32[]{:S(2)}) collective-permute-start(f32[15,8,768]{2,1,0:T(8,128)S(1)} %get-tuple-element.57), channel_id=1, source_target_pairs={{16,0},{32,16},{48,32},{64,48},{80,64},{96,80},{112,96},{128,112},... | collective-permute-start | bytes 1105928 | tf_op jit(solution)/shard_map/ppermute | solution.py:251
  54.2 9.7 %collective-permute-start.4 = (f32[15,8,768]{2,1,0:T(8,128)S(1)}, f32[15,8,768]{2,1,0:T(8,128)S(1)}, u32[]{:S(2)}, u32[]{:S(2)}) collective-permute-start(f32[15,8,768]{2,1,0:T(8,128)S(1)} %get-tuple-element.58), channel_id=1, source_target_pairs={{0,16},{16,32},{32,48},{48,64},{64,80},{80,96},{96,112},{112,128},... | collective-permute-start | bytes 1105928 | tf_op jit(solution)/shard_map/ppermute | solution.py:250
  60.1 3.8 %copy-start.5 = (f32[15,8,768]{2,1,0:T(8,128)}, f32[15,8,768]{2,1,0:T(8,128)S(1)}, u32[]{:S(2)}) copy-start(f32[15,8,768]{2,1,0:T(8,128)S(1)} %collective-permute-done.5.high_ref) | copy-start | bytes 1105924
  63.9 0.7 copy-start.9
  69.5 25.0 %collective-permute-start.7 = (f32[5,16,768]{2,1,0:T(8,128)}, f32[5,16,768]{2,1,0:T(8,128)}, u32[]{:S(2)}, u32[]{:S(2)}) collective-permute-start(f32[5,16,768]{2,1,0:T(8,128)} %get-tuple-element.55), channel_id=1, source_target_pairs={{1,0},{2,1},{3,2},{4,3},{5,4},{6,5},{7,6},{8,7},{9,8},{10,9},{11,1... | collective-permute-start | bytes 737288 | tf_op jit(solution)/shard_map/ppermute | solution.py:251
  71.7 22.7 %collective-permute-start.6 = (f32[5,16,768]{2,1,0:T(8,128)}, f32[5,16,768]{2,1,0:T(8,128)}, u32[]{:S(2)}, u32[]{:S(2)}) collective-permute-start(f32[5,16,768]{2,1,0:T(8,128)} %get-tuple-element.56), channel_id=1, source_target_pairs={{0,1},{1,2},{2,3},{3,4},{4,5},{5,6},{6,7},{7,8},{8,9},{9,10},{10,1... | collective-permute-start | bytes 737288 | tf_op jit(solution)/shard_map/ppermute | solution.py:250
  81.9 47.9 %all-to-all-start = ((f32[32,24,128]{2,1,0:T(8,128)}), f32[32,24,128]{2,1,0:T(8,128)S(1)}, u32[]{:S(2)}, u32[]{:S(2)}) async-start(f32[32,24,128]{2,1,0:T(8,128)} %copy.13), calls=%async_computation | async-start | bytes 786432 | tf_op jit(solution)/shard_map/all_to_all | solution.py:260
  99.6 13.3 %collective-permute-start.9 = (f32[5,16,768]{2,1,0:T(8,128)S(1)}, f32[5,16,768]{2,1,0:T(8,128)S(1)}, u32[]{:S(2)}, u32[]{:S(2)}) collective-permute-start(f32[5,16,768]{2,1,0:T(8,128)S(1)} %get-tuple-element.53), channel_id=1, source_target_pairs={{1,0},{2,1},{3,2},{4,3},{5,4},{6,5},{7,6},{8,7},{9,8},{10,9},{11,1... | collective-permute-start | bytes 737288 | tf_op jit(solution)/shard_map/ppermute | solution.py:251
  103.6 17.9 %collective-permute-start.8 = (f32[5,16,768]{2,1,0:T(8,128)S(1)}, f32[5,16,768]{2,1,0:T(8,128)S(1)}, u32[]{:S(2)}, u32[]{:S(2)}) collective-permute-start(f32[5,16,768]{2,1,0:T(8,128)S(1)} %get-tuple-element.54), channel_id=1, source_target_pairs={{0,1},{1,2},{2,3},{3,4},{4,5},{5,6},{6,7},{7,8},{8,9},{9,10},{10,1... | collective-permute-start | bytes 737288 | tf_op jit(solution)/shard_map/ppermute | solution.py:250
  112.9 8.6 %copy-start.16 = (f32[5,16,768]{2,1,0:T(8,128)}, f32[5,16,768]{2,1,0:T(8,128)S(1)}, u32[]{:S(2)}) copy-start(f32[5,16,768]{2,1,0:T(8,128)S(1)} %collective-permute-done.9.high_ref) | copy-start | bytes 737284
  121.5 0.7 copy-start.21
  125.5 5.3 %collective-permute-start.11 = (f32[5,8,768]{2,1,0:T(8,128)S(1)}, f32[5,8,768]{2,1,0:T(8,128)S(1)}, u32[]{:S(2)}, u32[]{:S(2)}) collective-permute-start(f32[5,8,768]{2,1,0:T(8,128)S(1)} %get-tuple-element.51), channel_id=1, source_target_pairs={{16,0},{32,16},{48,32},{64,48},{80,64},{96,80},{112,96},{128,112},... | collective-permute-start | bytes 368648 | tf_op jit(solution)/shard_map/ppermute | solution.py:251
  127.4 7.1 %collective-permute-start.10 = (f32[5,8,768]{2,1,0:T(8,128)S(1)}, f32[5,8,768]{2,1,0:T(8,128)S(1)}, u32[]{:S(2)}, u32[]{:S(2)}) collective-permute-start(f32[5,8,768]{2,1,0:T(8,128)S(1)} %get-tuple-element.52), channel_id=1, source_target_pairs={{0,16},{16,32},{32,48},{48,64},{64,80},{80,96},{96,112},{112,128},... | collective-permute-start | bytes 368648 | tf_op jit(solution)/shard_map/ppermute | solution.py:250
  130.8 3.7 %copy-start.24 = (f32[5,8,768]{2,1,0:T(8,128)}, f32[5,8,768]{2,1,0:T(8,128)S(1)}, u32[]{:S(2)}) copy-start(f32[5,8,768]{2,1,0:T(8,128)S(1)} %collective-permute-done.11.high_ref) | copy-start | bytes 368644
  134.5 0.6 copy-start.25
  138.6 4.4 %collective-permute-start.13 = (f32[5,8,768]{2,1,0:T(8,128)S(1)}, f32[5,8,768]{2,1,0:T(8,128)S(1)}, u32[]{:S(2)}, u32[]{:S(2)}) collective-permute-start(f32[5,8,768]{2,1,0:T(8,128)S(1)} %get-tuple-element.49), channel_id=1, source_target_pairs={{16,0},{32,16},{48,32},{64,48},{80,64},{96,80},{112,96},{128,112},... | collective-permute-start | bytes 368648 | tf_op jit(solution)/shard_map/ppermute | solution.py:251
  140.5 7.1 %collective-permute-start.12 = (f32[5,8,768]{2,1,0:T(8,128)S(1)}, f32[5,8,768]{2,1,0:T(8,128)S(1)}, u32[]{:S(2)}, u32[]{:S(2)}) collective-permute-start(f32[5,8,768]{2,1,0:T(8,128)S(1)} %get-tuple-element.50), channel_id=1, source_target_pairs={{0,16},{16,32},{32,48},{48,64},{64,80},{80,96},{96,112},{112,128},... | collective-permute-start | bytes 368648 | tf_op jit(solution)/shard_map/ppermute | solution.py:250
  142.9 4.7 %copy-start.28 = (f32[5,8,768]{2,1,0:T(8,128)}, f32[5,8,768]{2,1,0:T(8,128)S(1)}, u32[]{:S(2)}) copy-start(f32[5,8,768]{2,1,0:T(8,128)S(1)} %collective-permute-done.13.high_ref) | copy-start | bytes 368644
  151.6 13.4 %collective-permute-start.15 = (f32[5,16,768]{2,1,0:T(8,128)S(1)}, f32[5,16,768]{2,1,0:T(8,128)S(1)}, u32[]{:S(2)}, u32[]{:S(2)}) collective-permute-start(f32[5,16,768]{2,1,0:T(8,128)S(1)} %get-tuple-element.47), channel_id=1, source_target_pairs={{1,0},{2,1},{3,2},{4,3},{5,4},{6,5},{7,6},{8,7},{9,8},{10,9},{11,1... | collective-permute-start | bytes 737288 | tf_op jit(solution)/shard_map/ppermute | solution.py:251
  153.5 15.2 %collective-permute-start.14 = (f32[5,16,768]{2,1,0:T(8,128)S(1)}, f32[5,16,768]{2,1,0:T(8,128)S(1)}, u32[]{:S(2)}, u32[]{:S(2)}) collective-permute-start(f32[5,16,768]{2,1,0:T(8,128)S(1)} %get-tuple-element.48), channel_id=1, source_target_pairs={{0,1},{1,2},{2,3},{3,4},{4,5},{5,6},{6,7},{7,8},{8,9},{9,10},{10,1... | collective-permute-start | bytes 737288 | tf_op jit(solution)/shard_map/ppermute | solution.py:250
  164.9 3.8 %copy-start.11 = (f32[5,16,768]{2,1,0:T(8,128)}, f32[5,16,768]{2,1,0:T(8,128)S(1)}, u32[]{:S(2)}) copy-start(f32[5,16,768]{2,1,0:T(8,128)S(1)} %collective-permute-done.15.high_ref) | copy-start | bytes 737284
  168.7 0.7 copy-start.14
  174.5 13.6 %collective-permute-start.17 = (f32[5,16,768]{2,1,0:T(8,128)S(1)}, f32[5,16,768]{2,1,0:T(8,128)S(1)}, u32[]{:S(2)}, u32[]{:S(2)}) collective-permute-start(f32[5,16,768]{2,1,0:T(8,128)S(1)} %get-tuple-element.45), channel_id=1, source_target_pairs={{1,0},{2,1},{3,2},{4,3},{5,4},{6,5},{7,6},{8,7},{9,8},{10,9},{11,1... | collective-permute-start | bytes 737288 | tf_op jit(solution)/shard_map/ppermute | solution.py:251
  176.4 14.6 %collective-permute-start.16 = (f32[5,16,768]{2,1,0:T(8,128)S(1)}, f32[5,16,768]{2,1,0:T(8,128)S(1)}, u32[]{:S(2)}, u32[]{:S(2)}) collective-permute-start(f32[5,16,768]{2,1,0:T(8,128)S(1)} %get-tuple-element.46), channel_id=1, source_target_pairs={{0,1},{1,2},{2,3},{3,4},{4,5},{5,6},{6,7},{7,8},{8,9},{9,10},{10,1... | collective-permute-start | bytes 737288 | tf_op jit(solution)/shard_map/ppermute | solution.py:250
  188.1 3.0 copy-start.17
  191.1 0.7 copy-start.22
  195.2 7.6 %collective-permute-start.19 = (f32[15,8,768]{2,1,0:T(8,128)S(1)}, f32[15,8,768]{2,1,0:T(8,128)S(1)}, u32[]{:S(2)}, u32[]{:S(2)}) collective-permute-start(f32[15,8,768]{2,1,0:T(8,128)S(1)} %get-tuple-element.43), channel_id=1, source_target_pairs={{16,0},{32,16},{48,32},{64,48},{80,64},{96,80},{112,96},{128,112},... | collective-permute-start | bytes 1105928 | tf_op jit(solution)/shard_map/ppermute | solution.py:251
  197.2 9.7 %collective-permute-start.18 = (f32[15,8,768]{2,1,0:T(8,128)S(1)}, f32[15,8,768]{2,1,0:T(8,128)S(1)}, u32[]{:S(2)}, u32[]{:S(2)}) collective-permute-start(f32[15,8,768]{2,1,0:T(8,128)S(1)} %get-tuple-element.44), channel_id=1, source_target_pairs={{0,16},{16,32},{32,48},{48,64},{64,80},{80,96},{96,112},{112,128},... | collective-permute-start | bytes 1105928 | tf_op jit(solution)/shard_map/ppermute | solution.py:250
  202.8 4.1 %copy-start.3 = (f32[15,8,768]{2,1,0:T(8,128)}, f32[15,8,768]{2,1,0:T(8,128)S(1)}, u32[]{:S(2)}) copy-start(f32[15,8,768]{2,1,0:T(8,128)S(1)} %collective-permute-done.19.high_ref) | copy-start | bytes 1105924
  206.9 0.8 copy-start.7
  212.0 7.8 %collective-permute-start.21 = (f32[15,8,768]{2,1,0:T(8,128)S(1)}, f32[15,8,768]{2,1,0:T(8,128)S(1)}, u32[]{:S(2)}, u32[]{:S(2)}) collective-permute-start(f32[15,8,768]{2,1,0:T(8,128)S(1)} %get-tuple-element.41), channel_id=1, source_target_pairs={{16,0},{32,16},{48,32},{64,48},{80,64},{96,80},{112,96},{128,112},... | collective-permute-start | bytes 1105928 | tf_op jit(solution)/shard_map/ppermute | solution.py:251
  213.9 9.7 %collective-permute-start.20 = (f32[15,8,768]{2,1,0:T(8,128)S(1)}, f32[15,8,768]{2,1,0:T(8,128)S(1)}, u32[]{:S(2)}, u32[]{:S(2)}) collective-permute-start(f32[15,8,768]{2,1,0:T(8,128)S(1)} %get-tuple-element.42), channel_id=1, source_target_pairs={{0,16},{16,32},{32,48},{48,64},{64,80},{80,96},{96,112},{112,128},... | collective-permute-start | bytes 1105928 | tf_op jit(solution)/shard_map/ppermute | solution.py:250
  219.8 3.8 %copy-start.4 = (f32[15,8,768]{2,1,0:T(8,128)}, f32[15,8,768]{2,1,0:T(8,128)S(1)}, u32[]{:S(2)}) copy-start(f32[15,8,768]{2,1,0:T(8,128)S(1)} %collective-permute-done.21.high_ref) | copy-start | bytes 1105924
  223.7 0.7 copy-start.8
  228.4 16.0 %collective-permute-start.23 = (f32[5,16,768]{2,1,0:T(8,128)S(1)}, f32[5,16,768]{2,1,0:T(8,128)S(1)}, u32[]{:S(2)}, u32[]{:S(2)}) collective-permute-start(f32[5,16,768]{2,1,0:T(8,128)S(1)} %get-tuple-element.39), channel_id=1, source_target_pairs={{1,0},{2,1},{3,2},{4,3},{5,4},{6,5},{7,6},{8,7},{9,8},{10,9},{11,1... | collective-permute-start | bytes 737288 | tf_op jit(solution)/shard_map/ppermute | solution.py:251
  230.8 21.5 %collective-permute-start.22 = (f32[5,16,768]{2,1,0:T(8,128)S(1)}, f32[5,16,768]{2,1,0:T(8,128)S(1)}, u32[]{:S(2)}, u32[]{:S(2)}) collective-permute-start(f32[5,16,768]{2,1,0:T(8,128)S(1)} %get-tuple-element.40), channel_id=1, source_target_pairs={{0,1},{1,2},{2,3},{3,4},{4,5},{5,6},{6,7},{7,8},{8,9},{9,10},{10,1... | collective-permute-start | bytes 737288 | tf_op jit(solution)/shard_map/ppermute | solution.py:250
  244.5 7.9 %copy-start.10 = (f32[5,16,768]{2,1,0:T(8,128)}, f32[5,16,768]{2,1,0:T(8,128)S(1)}, u32[]{:S(2)}) copy-start(f32[5,16,768]{2,1,0:T(8,128)S(1)} %collective-permute-done.23.high_ref) | copy-start | bytes 737284
  252.3 0.7 copy-start.13
  258.1 9.8 %collective-permute-start.25 = (f32[5,16,768]{2,1,0:T(8,128)S(1)}, f32[5,16,768]{2,1,0:T(8,128)S(1)}, u32[]{:S(2)}, u32[]{:S(2)}) collective-permute-start(f32[5,16,768]{2,1,0:T(8,128)S(1)} %get-tuple-element.37), channel_id=1, source_target_pairs={{1,0},{2,1},{3,2},{4,3},{5,4},{6,5},{7,6},{8,7},{9,8},{10,9},{11,1... | collective-permute-start | bytes 737288 | tf_op jit(solution)/shard_map/ppermute | solution.py:251
  261.6 13.2 %collective-permute-start.24 = (f32[5,16,768]{2,1,0:T(8,128)S(1)}, f32[5,16,768]{2,1,0:T(8,128)S(1)}, u32[]{:S(2)}, u32[]{:S(2)}) collective-permute-start(f32[5,16,768]{2,1,0:T(8,128)S(1)} %get-tuple-element.38), channel_id=1, source_target_pairs={{0,1},{1,2},{2,3},{3,4},{4,5},{5,6},{6,7},{7,8},{8,9},{9,10},{10,1... | collective-permute-start | bytes 737288 | tf_op jit(solution)/shard_map/ppermute | solution.py:250
  267.9 6.8 %copy-start.18 = (f32[5,16,768]{2,1,0:T(8,128)}, f32[5,16,768]{2,1,0:T(8,128)S(1)}, u32[]{:S(2)}) copy-start(f32[5,16,768]{2,1,0:T(8,128)S(1)} %collective-permute-done.25.high_ref) | copy-start | bytes 737284
  274.8 0.7 copy-start.23
  278.8 4.4 %collective-permute-start.27 = (f32[5,8,768]{2,1,0:T(8,128)S(1)}, f32[5,8,768]{2,1,0:T(8,128)S(1)}, u32[]{:S(2)}, u32[]{:S(2)}) collective-permute-start(f32[5,8,768]{2,1,0:T(8,128)S(1)} %get-tuple-element.35), channel_id=1, source_target_pairs={{16,0},{32,16},{48,32},{64,48},{80,64},{96,80},{112,96},{128,112},... | collective-permute-start | bytes 368648 | tf_op jit(solution)/shard_map/ppermute | solution.py:251
  280.7 7.1 %collective-permute-start.26 = (f32[5,8,768]{2,1,0:T(8,128)S(1)}, f32[5,8,768]{2,1,0:T(8,128)S(1)}, u32[]{:S(2)}, u32[]{:S(2)}) collective-permute-start(f32[5,8,768]{2,1,0:T(8,128)S(1)} %get-tuple-element.36), channel_id=1, source_target_pairs={{0,16},{16,32},{32,48},{48,64},{64,80},{80,96},{96,112},{112,128},... | collective-permute-start | bytes 368648 | tf_op jit(solution)/shard_map/ppermute | solution.py:250
  283.1 4.7 %copy-start.26 = (f32[5,8,768]{2,1,0:T(8,128)}, f32[5,8,768]{2,1,0:T(8,128)S(1)}, u32[]{:S(2)}) copy-start(f32[5,8,768]{2,1,0:T(8,128)S(1)} %collective-permute-done.27.high_ref) | copy-start | bytes 368644
  287.8 0.6 copy-start.29
  291.8 4.4 %collective-permute-start.29 = (f32[5,8,768]{2,1,0:T(8,128)S(1)}, f32[5,8,768]{2,1,0:T(8,128)S(1)}, u32[]{:S(2)}, u32[]{:S(2)}) collective-permute-start(f32[5,8,768]{2,1,0:T(8,128)S(1)} %get-tuple-element.33), channel_id=1, source_target_pairs={{16,0},{32,16},{48,32},{64,48},{80,64},{96,80},{112,96},{128,112},... | collective-permute-start | bytes 368648 | tf_op jit(solution)/shard_map/ppermute | solution.py:251
  293.8 7.1 %collective-permute-start.28 = (f32[5,8,768]{2,1,0:T(8,128)S(1)}, f32[5,8,768]{2,1,0:T(8,128)S(1)}, u32[]{:S(2)}, u32[]{:S(2)}) collective-permute-start(f32[5,8,768]{2,1,0:T(8,128)S(1)} %get-tuple-element.34), channel_id=1, source_target_pairs={{0,16},{16,32},{32,48},{48,64},{64,80},{80,96},{96,112},{112,128},... | collective-permute-start | bytes 368648 | tf_op jit(solution)/shard_map/ppermute | solution.py:250
  296.2 4.7 %copy-start.27 = (f32[5,8,768]{2,1,0:T(8,128)}, f32[5,8,768]{2,1,0:T(8,128)S(1)}, u32[]{:S(2)}) copy-start(f32[5,8,768]{2,1,0:T(8,128)S(1)} %collective-permute-done.29.high_ref) | copy-start | bytes 368644
  300.9 0.6 copy-start.30
  304.9 14.5 %collective-permute-start.31 = (f32[5,16,768]{2,1,0:T(8,128)S(1)}, f32[5,16,768]{2,1,0:T(8,128)S(1)}, u32[]{:S(2)}, u32[]{:S(2)}) collective-permute-start(f32[5,16,768]{2,1,0:T(8,128)S(1)} %get-tuple-element.31), channel_id=1, source_target_pairs={{1,0},{2,1},{3,2},{4,3},{5,4},{6,5},{7,6},{8,7},{9,8},{10,9},{11,1... | collective-permute-start | bytes 737288 | tf_op jit(solution)/shard_map/ppermute | solution.py:251
  313.1 13.0 %collective-permute-start.30 = (f32[5,16,768]{2,1,0:T(8,128)S(1)}, f32[5,16,768]{2,1,0:T(8,128)S(1)}, u32[]{:S(2)}, u32[]{:S(2)}) collective-permute-start(f32[5,16,768]{2,1,0:T(8,128)S(1)} %get-tuple-element.32), channel_id=1, source_target_pairs={{0,1},{1,2},{2,3},{3,4},{4,5},{5,6},{6,7},{7,8},{8,9},{9,10},{10,1... | collective-permute-start | bytes 737288 | tf_op jit(solution)/shard_map/ppermute | solution.py:250
  319.4 6.7 %copy-start.12 = (f32[5,16,768]{2,1,0:T(8,128)}, f32[5,16,768]{2,1,0:T(8,128)S(1)}, u32[]{:S(2)}) copy-start(f32[5,16,768]{2,1,0:T(8,128)S(1)} %collective-permute-done.31.high_ref) | copy-start | bytes 737284
  326.1 0.7 copy-start.19
  (1 other events, 0.6 us)

commit v2 on v1

v2 whole, which is shorter than its diff:
```python
import functools
import jax
import jax.numpy as jnp
from jax import lax
from jax.experimental import pallas as pl
from jax.experimental.pallas import tpu as pltpu
from jax.sharding import PartitionSpec as P

ITERS = 2
LANES = 128
SHIFT = 64
CHUNKS = 1
CHUNK_LIMIT = 8 * 2**20
HIGH = lax.Precision.HIGHEST
VMEM = pl.BlockSpec(memory_space=pltpu.VMEM)
LIMIT = pltpu.CompilerParams(vmem_limit_bytes=CHUNK_LIMIT)
SMEM = pl.BlockSpec(memory_space=pltpu.SMEM)


def splat(value):
    return jnp.full((8, LANES), value, jnp.float32)


def prepare_body(axial_ref, lateral_ref, ya_ref, yb_ref, za_ref, zb_ref, *band_refs):
    axial, lateral = axial_ref.shape[1], lateral_ref.shape[2]

    def normalized(read, count):
        taps = [read(k) for k in range(count)]
        total = taps[0]
        for tap in taps[1:]:
            total = total + tap
        total = splat(total)
        return [splat(tap) / total for tap in taps]

    rows = (
        (ya_ref, lambda k: axial_ref[0, k], axial),
        (yb_ref, lambda k: lateral_ref[1, 1, k], lateral),
        (za_ref, lambda k: lateral_ref[0, 0, k], lateral),
        (zb_ref, lambda k: lateral_ref[1, 0, k], lateral),
    )
    for target, read, count in rows:
        for k, tap in enumerate(normalized(read, count)):
            target[k] = tap
    xa = normalized(lambda k: lateral_ref[0, 1, k], lateral)
    xb = normalized(lambda k: axial_ref[1, k], axial)
    lane = lax.broadcasted_iota(jnp.int32, (8, LANES), 1)
    sub = lax.broadcasted_iota(jnp.int32, (8, LANES), 0)

    def fill(step, carry):
        distance = sub + step * 8 - lane - SHIFT
        for index, taps in enumerate((xa, xb)):
            half = len(taps) // 2
            ahead = jnp.zeros((8, LANES), jnp.float32)
            back = jnp.zeros((8, LANES), jnp.float32)
            for k, tap in enumerate(taps):
                ahead = jnp.where(distance == k - half, tap, ahead)
                back = jnp.where(distance == half - k, tap, back)
            at = pl.ds(pl.multiple_of(step * 8, 8), 8)
            band_refs[2 * index][at, :] = ahead
            band_refs[2 * index + 1][at, :] = back
        return carry

    lax.fori_loop(0, 2 * LANES // 8, fill, 0)


def local(*shape):
    return pltpu.VMEM(shape, jnp.float32)


def call(body, name, operands, shapes, scratch=()):
    operands = [pltpu.with_memory_space_constraint(operand, pltpu.VMEM) for operand in operands]
    return pl.pallas_call(
        body,
        out_shape=shapes,
        in_specs=[VMEM] * len(operands),
        out_specs=[VMEM] * len(shapes),
        scratch_shapes=scratch,
        compiler_params=LIMIT,
        name=name,
    )(*operands)


def prepare(axial_kernel, lateral_kernel):
    axial, lateral = axial_kernel.shape[1], lateral_kernel.shape[2]
    shapes = [local(count, 8, LANES) for count in (axial, lateral, lateral, lateral)]
    shapes += [local(2 * LANES, LANES)] * 4
    outs = pl.pallas_call(
        prepare_body,
        out_shape=shapes,
        in_specs=[SMEM, SMEM],
        out_specs=[VMEM] * len(shapes),
        compiler_params=LIMIT,
        name="prepare",
    )(axial_kernel, lateral_kernel)
    return outs[:2], outs[2:4], (outs[4:6], outs[6:8])


def correlate(taps, rows, extent, reverse):
    count = len(taps)
    sums = [None] * extent
    for r in range(extent + count - 1):
        value = rows(r)
        for i in range(max(0, r - count + 1), min(extent, r + 1)):
            k = r - i
            term = taps[count - 1 - k if reverse else k] * value
            sums[i] = term if sums[i] is None else sums[i] + term
    return sums


def padded_rows(low, mid, high, pick):
    margin, extent = low.shape[0], mid.shape[0]

    def rows(r):
        if r < margin:
            return pick(low, r)
        if r < margin + extent:
            return pick(mid, r - margin)
        return pick(high, r - margin - extent)

    return rows


def lanes_at(j):
    return pl.ds(pl.multiple_of(j * LANES, LANES), LANES)


def put(out_refs, i, at, lanes, value):
    mid_ref, first_ref, last_ref = out_refs
    extent, margin = mid_ref.shape[0], first_ref.shape[0]
    mid_ref[i, at, lanes] = value
    if i < margin:
        first_ref[i, at, lanes] = value
    if i >= extent - margin:
        last_ref[i - extent + margin, at, lanes] = value


def along_z(taps_ref, low_ref, mid_ref, high_ref, reverse, store):
    rows_y, width = mid_ref.shape[1], mid_ref.shape[2]

    def tile(j, carry):
        lanes = lanes_at(j)
        taps = [taps_ref[k] for k in range(taps_ref.shape[0])]
        for y in range(0, rows_y, 8):
            pick = lambda ref, r: ref[r, y:y + 8, lanes]
            sums = correlate(taps, padded_rows(low_ref, mid_ref, high_ref, pick), mid_ref.shape[0], reverse)
            store(y, j, sums)
        return carry

    lax.fori_loop(0, width // LANES, tile, 0)


def depth_body(reverse, taps_ref, low_ref, mid_ref, high_ref, *out_refs):
    def store(y, j, sums):
        turned = jnp.swapaxes(jnp.stack(sums), 0, 1)
        for i in range(8):
            put(out_refs, y + i, slice(None), lanes_at(j), turned[i])

    along_z(taps_ref, low_ref, mid_ref, high_ref, reverse, store)


def depth(taps, low, mid, high, reverse, margin):
    nz, ny, nx = mid.shape
    shapes = [local(ny, nz, nx), local(margin, nz, nx), local(margin, nz, nx)]
    return call(functools.partial(depth_body, reverse), "depth", (taps, low, mid, high), shapes)


def plane_body(reverse, divide, taps_ref, low_ref, mid_ref, high_ref, *refs):
    view_ref, out_refs = (refs[0], refs[1:]) if divide else (None, refs)

    def tile(j, carry):
        lanes = lanes_at(j)
        taps = [taps_ref[k] for k in range(taps_ref.shape[0])]
        pick = lambda ref, r: ref[r, :, lanes]
        sums = correlate(taps, padded_rows(low_ref, mid_ref, high_ref, pick), mid_ref.shape[0], reverse)
        if divide:
            for i, value in enumerate(sums):
                put(out_refs, i, slice(None), lanes, view_ref[i, :, lanes] / value)
        else:
            for y in range(0, len(sums), 8):
                turned = jnp.swapaxes(jnp.stack(sums[y:y + 8]), 0, 1)
                for z in range(8):
                    put(out_refs, z, slice(y, y + 8), lanes, turned[z])
        return carry

    lax.fori_loop(0, mid_ref.shape[2] // LANES, tile, 0)


def plane(taps, low, mid, high, reverse, margin, view=None):
    ny, nz, nx = mid.shape
    outer, inner = (nz, ny) if view is None else (ny, nz)
    shapes = [local(outer, inner, nx), local(margin, inner, nx), local(margin, inner, nx)]
    operands = (taps, low, mid, high) + (() if view is None else (view,))
    return call(functools.partial(plane_body, reverse, view is not None), "plane", operands, shapes)


def clear_edges(wide_ref):
    blank = jnp.zeros((wide_ref.shape[0], LANES), jnp.float32)
    wide_ref[:, :LANES] = blank
    wide_ref[:, wide_ref.shape[1] - LANES:] = blank


def along_x(wide_ref, band):
    width = wide_ref.shape[1] - LANES
    for j in range(width // LANES):
        yield j, jnp.dot(
            wide_ref[:, j * LANES:(j + 2) * LANES], band, precision=HIGH, preferred_element_type=jnp.float32
        )


def put_ahead(wide_ref, band_ref, out_refs, ny):
    per_chunk = out_refs[0].shape[2] // LANES
    for j, value in along_x(wide_ref, band_ref[...]):
        chunk, inside = divmod(j, per_chunk)
        refs = out_refs[3 * chunk:3 * chunk + 3]
        lanes = slice(inside * LANES, (inside + 1) * LANES)
        for z in range(refs[0].shape[0]):
            put(refs, z, slice(None), lanes, value[z * ny:(z + 1) * ny])


def first_body(band_ref, estimate_ref, *refs):
    out_refs, wide_ref = refs[:-1], refs[-1]
    nz, ny, nx = estimate_ref.shape
    clear_edges(wide_ref)
    wide_ref[:, SHIFT:SHIFT + nx] = estimate_ref[...].reshape(nz * ny, nx)
    put_ahead(wide_ref, band_ref, out_refs, ny)


def ahead_shapes(shape, margin):
    nz, ny, nx = shape
    part = nx // CHUNKS
    return [local(nz, ny, part), local(margin, ny, part), local(margin, ny, part)] * CHUNKS


def chunked(outs):
    return [tuple(outs[3 * c:3 * c + 3]) for c in range(CHUNKS)]


def first(band, estimate, margin):
    nz, ny, nx = estimate.shape
    shapes = ahead_shapes(estimate.shape, margin)
    scratch = [local(nz * ny, nx + LANES)]
    return chunked(call(first_body, "first", (band, estimate), shapes, scratch))


def update_body(last, taps_ref, band_ref, estimate_ref, *refs):
    halo_refs, refs = refs[:3 * CHUNKS], refs[3 * CHUNKS:]
    refs, (wide_ref, mixed_ref) = refs[:-2], refs[-2:]
    if last:
        (out_ref,) = refs
    else:
        next_ref, out_ref, *ahead_refs = refs
    nz, ny, nx = estimate_ref.shape
    per_chunk = nx // CHUNKS // LANES
    for c in range(CHUNKS):
        def store(y, j, sums):
            for z, value in enumerate(sums):
                mixed_ref[z * ny + y:z * ny + y + 8, lanes_at(j + c * per_chunk)] = value

        along_z(taps_ref, *halo_refs[3 * c:3 * c + 3], True, store)
    clear_edges(wide_ref)
    wide_ref[:, SHIFT:SHIFT + nx] = mixed_ref[...]
    for j, value in along_x(wide_ref, band_ref[...]):
        at = slice(j * LANES, (j + 1) * LANES)
        out_ref[:, :, at] = estimate_ref[:, :, at] * value.reshape(nz, ny, LANES)
    if not last:
        wide_ref[:, SHIFT:SHIFT + nx] = out_ref[...].reshape(nz * ny, nx)
        put_ahead(wide_ref, next_ref, ahead_refs, ny)


def update(taps, halos, band, estimate, band_next=None):
    nz, ny, nx = estimate.shape
    last = band_next is None
    operands = (taps, band, estimate) + sum(halos, ()) + (() if last else (band_next,))
    shapes = [local(nz, ny, nx)]
    if last:
        shapes = [jax.ShapeDtypeStruct((nz, ny, nx), jnp.float32)]
    else:
        shapes += ahead_shapes(estimate.shape, taps.shape[0] // 2)
    scratch = [local(nz * ny, nx + LANES), local(nz * ny, nx)]
    outs = call(functools.partial(update_body, last), "update", operands, shapes, scratch)
    return outs[0], (None if last else chunked(outs[1:]))


def exchange(parts, axis):
    block, first_rows, last_rows = parts
    count = lax.axis_size(axis)
    forward = [(i, i + 1) for i in range(count - 1)]
    backward = [(target, source) for source, target in forward]
    low = lax.ppermute(last_rows, axis, forward)
    high = lax.ppermute(first_rows, axis, backward)
    return low, block, high


def reframe(view):
    nz, nx, ny = view.shape
    count = lax.axis_size("row")
    rows = ny // count
    pieces = view.reshape(nz, nx, count, rows).transpose(2, 1, 3, 0).reshape(count, nx, rows * nz)
    arrived = lax.all_to_all(pieces, "row", 0, 0, tiled=True)
    return arrived.reshape(count * nx, rows * nz).T.reshape(rows, nz, count * nx)


def per_device(view_a, view_b, estimate, axial_kernel, lateral_kernel):
    ytaps, ztaps, bands = prepare(axial_kernel, lateral_kernel)
    views = (jnp.swapaxes(view_a, 0, 1), reframe(view_b))
    views = [jnp.split(view, CHUNKS, axis=2) for view in views]
    depth_margin = lateral_kernel.shape[2] // 2
    ahead = first(bands[0][0], estimate, depth_margin)
    steps = 2 * ITERS
    for step in range(steps):
        v = step % 2
        yt, zt = ytaps[v], ztaps[v]
        margin = yt.shape[0] // 2
        ahead = [depth(zt, *exchange(parts, "col"), False, margin) for parts in ahead]
        ahead = [
            plane(yt, *exchange(parts, "row"), False, margin, view) for parts, view in zip(ahead, views[v])
        ]
        ahead = [plane(yt, *exchange(parts, "row"), True, depth_margin) for parts in ahead]
        halos = [exchange(parts, "col") for parts in ahead]
        band_next = None if step == steps - 1 else bands[1 - v][0]
        estimate, ahead = update(zt, halos, bands[v][1], estimate, band_next)
    return estimate


def solution(mesh):
    in_specs = (P("col", "row", None), P("col", "row", None), P("col", "row", None), P(), P())
    out_specs = P("col", "row", None)
    return jax.shard_map(
        per_device, mesh=mesh, in_specs=in_specs, out_specs=out_specs, check_vma=False
    )
```

time: 332 us -> 283 us (0.85)
  the two profiles are of different devices: /device:TPU:68 before, /device:TPU:121 now
where the time goes in v2:
time: 283 us; the launch traced here: 282 us
  waiting for transfers between devices  145 us (51%)
  starting transfers between devices  107 us (38%)
  Pallas kernels  16.7 us (6%)
  local copies, waits for them, and re-layouts  13.4 us (5%)
    ppermute x16, waiting for transfers between devices, exchange(): low = lax.ppermute(last_rows, axis, forward)  79.4 us
    ppermute x16, waiting for transfers between devices, exchange(): high = lax.ppermute(first_rows, axis, backward)  65.7 us
    ppermute x16, starting transfers between devices, exchange(): low = lax.ppermute(last_rows, axis, forward)  51.6 us
    ppermute x16, starting transfers between devices, exchange(): high = lax.ppermute(first_rows, axis, backward)  43.3 us
    pallas_call x17, Pallas kernels, call(): pl.pallas_call(body, out_shape=shapes, in_specs=[VMEM] * len(operands), o...  15.1 us
    all_to_all x1, starting transfers between devices, reframe(): arrived = lax.all_to_all(pieces, 'row', 0, 0, tiled=True)  11.6 us
  transfers between devices with their start and end apart: 33, of which 26 were waited for; matrix products, arithmetic and copies ran while one was open for 4% of the time, Pallas kernels for 1%

profile of v2, /device:TPU:121, one launch (start us, length us, event | category | flops | bytes accessed | tf_op | source)
XLA Modules:
  0.0 282.2 jit_solution(9333662243956835427)
XLA Ops:
  4.8 3.3 %collective-permute-start = (f32[5,16,768]{2,1,0:T(8,128)S(1)}, f32[5,16,768]{2,1,0:T(8,128)S(1)}, u32[]{:S(2)}, u32[]{:S(2)}) collective-permute-start(f32[5,16,768]{2,1,0:T(8,128)S(1)} %get-tuple-element.70), channel_id=1, source_target_pairs={{0,1},{1,2},{2,3},{3,4},{4,5},{5,6},{6,7},{7,8},{8,9},{9,10},{10,1... | collective-permute-start | bytes 737288 | tf_op jit(solution)/shard_map/ppermute | solution.py:289
  8.1 2.8 %collective-permute-start.1 = (f32[5,16,768]{2,1,0:T(8,128)S(1)}, f32[5,16,768]{2,1,0:T(8,128)S(1)}, u32[]{:S(2)}, u32[]{:S(2)}) collective-permute-start(f32[5,16,768]{2,1,0:T(8,128)S(1)} %get-tuple-element.72), channel_id=1, source_target_pairs={{1,0},{2,1},{3,2},{4,3},{5,4},{6,5},{7,6},{8,7},{9,8},{10,9},{11,1... | collective-permute-start | bytes 737288 | tf_op jit(solution)/shard_map/ppermute | solution.py:290
  10.9 8.9 %collective-permute-done.low_ref = f32[5,16,768]{2,1,0:T(8,128)S(1)} collective-permute-done((f32[5,16,768]{2,1,0:T(8,128)S(1)}, f32[5,16,768]{2,1,0:T(8,128)S(1)}, u32[]{:S(2)}, u32[]{:S(2)}) %collective-permute-start) | collective-permute-done | bytes 245792 | tf_op jit(solution)/shard_map/ppermute | solution.py:289
  21.7 9.1 %collective-permute-start.2 = (f32[15,8,768]{2,1,0:T(8,128)S(1)}, f32[15,8,768]{2,1,0:T(8,128)S(1)}, u32[]{:S(2)}, u32[]{:S(2)}) collective-permute-start(f32[15,8,768]{2,1,0:T(8,128)S(1)} %get-tuple-element.73), channel_id=1, source_target_pairs={{0,16},{16,32},{32,48},{48,64},{64,80},{80,96},{96,112},{112,128},... | collective-permute-start | bytes 1105928 | tf_op jit(solution)/shard_map/ppermute | solution.py:289
  30.8 1.9 collective-permute-start.3
  34.0 4.4 %collective-permute-done.2.low_ref = f32[15,8,768]{2,1,0:T(8,128)S(1)} collective-permute-done((f32[15,8,768]{2,1,0:T(8,128)S(1)}, f32[15,8,768]{2,1,0:T(8,128)S(1)}, u32[]{:S(2)}, u32[]{:S(2)}) %collective-permute-start.2) | collective-permute-done | bytes 368672 | tf_op jit(solution)/shard_map/ppermute | solution.py:289
  38.4 2.2 collective-permute-done.3.high_ref
  41.6 3.1 %collective-permute-start.4 = (f32[15,8,768]{2,1,0:T(8,128)S(1)}, f32[15,8,768]{2,1,0:T(8,128)S(1)}, u32[]{:S(2)}, u32[]{:S(2)}) collective-permute-start(f32[15,8,768]{2,1,0:T(8,128)S(1)} %get-tuple-element.76), channel_id=1, source_target_pairs={{0,16},{16,32},{32,48},{48,64},{64,80},{80,96},{96,112},{112,128},... | collective-permute-start | bytes 1105928 | tf_op jit(solution)/shard_map/ppermute | solution.py:289
  44.7 1.9 collective-permute-start.5
  46.7 2.7 reshape.12
  49.4 3.3 %copy.12 = f32[32,24,16,8]{0,3,2,1:T(8,128)} copy(f32[32,24,16,8]{2,0,1,3:T(8,128)} %bitcast.13) | data formatting | bytes 786432 | tf_op jit(solution)/shard_map/transpose | solution.py:298
  52.6 2.6 copy.13
  55.3 11.6 %all-to-all-start = ((f32[32,24,128]{2,1,0:T(8,128)}), f32[32,24,128]{2,1,0:T(8,128)}, u32[]{:S(2)}, u32[]{:S(2)}) async-start(f32[32,24,128]{2,1,0:T(8,128)} %copy.13), calls=%async_computation | async-start | bytes 786432 | tf_op jit(solution)/shard_map/all_to_all | solution.py:299
  67.9 4.3 %collective-permute-start.6 = (f32[5,16,768]{2,1,0:T(8,128)S(1)}, f32[5,16,768]{2,1,0:T(8,128)S(1)}, u32[]{:S(2)}, u32[]{:S(2)}) collective-permute-start(f32[5,16,768]{2,1,0:T(8,128)S(1)} %get-tuple-element.79), channel_id=1, source_target_pairs={{0,1},{1,2},{2,3},{3,4},{4,5},{5,6},{6,7},{7,8},{8,9},{9,10},{10,1... | collective-permute-start | bytes 737288 | tf_op jit(solution)/shard_map/ppermute | solution.py:289
  72.2 1.9 collective-permute-start.7
  74.1 9.4 %collective-permute-done.6.refs_0_ = f32[5,16,768]{2,1,0:T(8,128)S(1)} collective-permute-done((f32[5,16,768]{2,1,0:T(8,128)S(1)}, f32[5,16,768]{2,1,0:T(8,128)S(1)}, u32[]{:S(2)}, u32[]{:S(2)}) %collective-permute-start.6) | collective-permute-done | bytes 245792 | tf_op jit(solution)/shard_map/ppermute | solution.py:289
  83.5 6.4 %collective-permute-done.7.refs_2_ = f32[5,16,768]{2,1,0:T(8,128)S(1)} collective-permute-done((f32[5,16,768]{2,1,0:T(8,128)S(1)}, f32[5,16,768]{2,1,0:T(8,128)S(1)}, u32[]{:S(2)}, u32[]{:S(2)}) %collective-permute-start.7) | collective-permute-done | bytes 245792 | tf_op jit(solution)/shard_map/ppermute | solution.py:290
  89.9 1.8 update.4
  91.7 1.9 collective-permute-start.8
  93.6 4.3 %collective-permute-start.9 = (f32[5,16,768]{2,1,0:T(8,128)S(1)}, f32[5,16,768]{2,1,0:T(8,128)S(1)}, u32[]{:S(2)}, u32[]{:S(2)}) collective-permute-start(f32[5,16,768]{2,1,0:T(8,128)S(1)} %get-tuple-element.87), channel_id=1, source_target_pairs={{1,0},{2,1},{3,2},{4,3},{5,4},{6,5},{7,6},{8,7},{9,8},{10,9},{11,1... | collective-permute-start | bytes 737288 | tf_op jit(solution)/shard_map/ppermute | solution.py:290
  97.9 9.0 %collective-permute-done.8.low_ref = f32[5,16,768]{2,1,0:T(8,128)S(1)} collective-permute-done((f32[5,16,768]{2,1,0:T(8,128)S(1)}, f32[5,16,768]{2,1,0:T(8,128)S(1)}, u32[]{:S(2)}, u32[]{:S(2)}) %collective-permute-start.8) | collective-permute-done | bytes 245792 | tf_op jit(solution)/shard_map/ppermute | solution.py:289
  106.9 4.0 %collective-permute-done.9.high_ref = f32[5,16,768]{2,1,0:T(8,128)S(1)} collective-permute-done((f32[5,16,768]{2,1,0:T(8,128)S(1)}, f32[5,16,768]{2,1,0:T(8,128)S(1)}, u32[]{:S(2)}, u32[]{:S(2)}) %collective-permute-start.9) | collective-permute-done | bytes 245792 | tf_op jit(solution)/shard_map/ppermute | solution.py:290
  111.3 1.9 collective-permute-start.10
  113.2 2.4 collective-permute-start.11
  116.8 3.5 %collective-permute-done.11.high_ref = f32[5,8,768]{2,1,0:T(8,128)S(1)} collective-permute-done((f32[5,8,768]{2,1,0:T(8,128)S(1)}, f32[5,8,768]{2,1,0:T(8,128)S(1)}, u32[]{:S(2)}, u32[]{:S(2)}) %collective-permute-start.11) | collective-permute-done | bytes 122912 | tf_op jit(solution)/shard_map/ppermute | solution.py:290
  120.7 1.9 collective-permute-start.12
  122.6 2.4 collective-permute-start.13
  125.0 4.7 %collective-permute-done.13.high_ref = f32[5,8,768]{2,1,0:T(8,128)S(1)} collective-permute-done((f32[5,8,768]{2,1,0:T(8,128)S(1)}, f32[5,8,768]{2,1,0:T(8,128)S(1)}, u32[]{:S(2)}, u32[]{:S(2)}) %collective-permute-start.13) | collective-permute-done | bytes 122912 | tf_op jit(solution)/shard_map/ppermute | solution.py:290
  130.1 1.9 collective-permute-start.14
  132.1 4.3 %collective-permute-start.15 = (f32[5,16,768]{2,1,0:T(8,128)S(1)}, f32[5,16,768]{2,1,0:T(8,128)S(1)}, u32[]{:S(2)}, u32[]{:S(2)}) collective-permute-start(f32[5,16,768]{2,1,0:T(8,128)S(1)} %get-tuple-element.96), channel_id=1, source_target_pairs={{1,0},{2,1},{3,2},{4,3},{5,4},{6,5},{7,6},{8,7},{9,8},{10,9},{11,1... | collective-permute-start | bytes 737288 | tf_op jit(solution)/shard_map/ppermute | solution.py:290
  136.3 8.6 %collective-permute-done.14.refs_0_ = f32[5,16,768]{2,1,0:T(8,128)S(1)} collective-permute-done((f32[5,16,768]{2,1,0:T(8,128)S(1)}, f32[5,16,768]{2,1,0:T(8,128)S(1)}, u32[]{:S(2)}, u32[]{:S(2)}) %collective-permute-start.14) | collective-permute-done | bytes 245792 | tf_op jit(solution)/shard_map/ppermute | solution.py:289
  145.0 3.0 %collective-permute-done.15.refs_2_ = f32[5,16,768]{2,1,0:T(8,128)S(1)} collective-permute-done((f32[5,16,768]{2,1,0:T(8,128)S(1)}, f32[5,16,768]{2,1,0:T(8,128)S(1)}, u32[]{:S(2)}, u32[]{:S(2)}) %collective-permute-start.15) | collective-permute-done | bytes 245792 | tf_op jit(solution)/shard_map/ppermute | solution.py:290
  149.7 1.9 collective-permute-start.16
  151.6 4.3 %collective-permute-start.17 = (f32[5,16,768]{2,1,0:T(8,128)S(1)}, f32[5,16,768]{2,1,0:T(8,128)S(1)}, u32[]{:S(2)}, u32[]{:S(2)}) collective-permute-start(f32[5,16,768]{2,1,0:T(8,128)S(1)} %get-tuple-element.100), channel_id=1, source_target_pairs={{1,0},{2,1},{3,2},{4,3},{5,4},{6,5},{7,6},{8,7},{9,8},{10,9},{11,1... | collective-permute-start | bytes 737288 | tf_op jit(solution)/shard_map/ppermute | solution.py:290
  155.9 7.8 %collective-permute-done.16.low_ref = f32[5,16,768]{2,1,0:T(8,128)S(1)} collective-permute-done((f32[5,16,768]{2,1,0:T(8,128)S(1)}, f32[5,16,768]{2,1,0:T(8,128)S(1)}, u32[]{:S(2)}, u32[]{:S(2)}) %collective-permute-start.16) | collective-permute-done | bytes 245792 | tf_op jit(solution)/shard_map/ppermute | solution.py:289
  163.7 6.0 %collective-permute-done.17.high_ref = f32[5,16,768]{2,1,0:T(8,128)S(1)} collective-permute-done((f32[5,16,768]{2,1,0:T(8,128)S(1)}, f32[5,16,768]{2,1,0:T(8,128)S(1)}, u32[]{:S(2)}, u32[]{:S(2)}) %collective-permute-start.17) | collective-permute-done | bytes 245792 | tf_op jit(solution)/shard_map/ppermute | solution.py:290
  170.1 3.6 %collective-permute-start.18 = (f32[15,8,768]{2,1,0:T(8,128)S(1)}, f32[15,8,768]{2,1,0:T(8,128)S(1)}, u32[]{:S(2)}, u32[]{:S(2)}) collective-permute-start(f32[15,8,768]{2,1,0:T(8,128)S(1)} %get-tuple-element.101), channel_id=1, source_target_pairs={{0,16},{16,32},{32,48},{48,64},{64,80},{80,96},{96,112},{112,128},... | collective-permute-start | bytes 1105928 | tf_op jit(solution)/shard_map/ppermute | solution.py:289
  173.7 1.9 collective-permute-start.19
  175.6 3.8 %collective-permute-done.18.low_ref = f32[15,8,768]{2,1,0:T(8,128)S(1)} collective-permute-done((f32[15,8,768]{2,1,0:T(8,128)S(1)}, f32[15,8,768]{2,1,0:T(8,128)S(1)}, u32[]{:S(2)}, u32[]{:S(2)}) %collective-permute-start.18) | collective-permute-done | bytes 368672 | tf_op jit(solution)/shard_map/ppermute | solution.py:289
  179.4 4.0 %collective-permute-done.19.high_ref = f32[15,8,768]{2,1,0:T(8,128)S(1)} collective-permute-done((f32[15,8,768]{2,1,0:T(8,128)S(1)}, f32[15,8,768]{2,1,0:T(8,128)S(1)}, u32[]{:S(2)}, u32[]{:S(2)}) %collective-permute-start.19) | collective-permute-done | bytes 368672 | tf_op jit(solution)/shard_map/ppermute | solution.py:290
  184.4 1.9 collective-permute-start.20
  186.4 2.4 collective-permute-start.21
  188.8 2.9 %collective-permute-done.20.low_ref = f32[15,8,768]{2,1,0:T(8,128)S(1)} collective-permute-done((f32[15,8,768]{2,1,0:T(8,128)S(1)}, f32[15,8,768]{2,1,0:T(8,128)S(1)}, u32[]{:S(2)}, u32[]{:S(2)}) %collective-permute-start.20) | collective-permute-done | bytes 368672 | tf_op jit(solution)/shard_map/ppermute | solution.py:289
  191.7 5.7 %collective-permute-done.21.high_ref = f32[15,8,768]{2,1,0:T(8,128)S(1)} collective-permute-done((f32[15,8,768]{2,1,0:T(8,128)S(1)}, f32[15,8,768]{2,1,0:T(8,128)S(1)}, u32[]{:S(2)}, u32[]{:S(2)}) %collective-permute-start.21) | collective-permute-done | bytes 368672 | tf_op jit(solution)/shard_map/ppermute | solution.py:290
  198.4 1.9 collective-permute-start.22
  200.3 4.3 %collective-permute-start.23 = (f32[5,16,768]{2,1,0:T(8,128)S(1)}, f32[5,16,768]{2,1,0:T(8,128)S(1)}, u32[]{:S(2)}, u32[]{:S(2)}) collective-permute-start(f32[5,16,768]{2,1,0:T(8,128)S(1)} %get-tuple-element.109), channel_id=1, source_target_pairs={{1,0},{2,1},{3,2},{4,3},{5,4},{6,5},{7,6},{8,7},{9,8},{10,9},{11,1... | collective-permute-start | bytes 737288 | tf_op jit(solution)/shard_map/ppermute | solution.py:290
  204.6 8.1 %collective-permute-done.22.refs_0_ = f32[5,16,768]{2,1,0:T(8,128)S(1)} collective-permute-done((f32[5,16,768]{2,1,0:T(8,128)S(1)}, f32[5,16,768]{2,1,0:T(8,128)S(1)}, u32[]{:S(2)}, u32[]{:S(2)}) %collective-permute-start.22) | collective-permute-done | bytes 245792 | tf_op jit(solution)/shard_map/ppermute | solution.py:289
  212.7 3.6 %collective-permute-done.23.refs_2_ = f32[5,16,768]{2,1,0:T(8,128)S(1)} collective-permute-done((f32[5,16,768]{2,1,0:T(8,128)S(1)}, f32[5,16,768]{2,1,0:T(8,128)S(1)}, u32[]{:S(2)}, u32[]{:S(2)}) %collective-permute-start.23) | collective-permute-done | bytes 245792 | tf_op jit(solution)/shard_map/ppermute | solution.py:290
  216.3 1.8 update.6
  218.1 5.6 %collective-permute-start.24 = (f32[5,16,768]{2,1,0:T(8,128)S(1)}, f32[5,16,768]{2,1,0:T(8,128)S(1)}, u32[]{:S(2)}, u32[]{:S(2)}) collective-permute-start(f32[5,16,768]{2,1,0:T(8,128)S(1)} %get-tuple-element.111), channel_id=1, source_target_pairs={{0,1},{1,2},{2,3},{3,4},{4,5},{5,6},{6,7},{7,8},{8,9},{9,10},{10,1... | collective-permute-start | bytes 737288 | tf_op jit(solution)/shard_map/ppermute | solution.py:289
  223.7 1.9 collective-permute-start.25
  225.6 8.2 %collective-permute-done.24.low_ref = f32[5,16,768]{2,1,0:T(8,128)S(1)} collective-permute-done((f32[5,16,768]{2,1,0:T(8,128)S(1)}, f32[5,16,768]{2,1,0:T(8,128)S(1)}, u32[]{:S(2)}, u32[]{:S(2)}) %collective-permute-start.24) | collective-permute-done | bytes 245792 | tf_op jit(solution)/shard_map/ppermute | solution.py:289
  233.8 5.8 %collective-permute-done.25.high_ref = f32[5,16,768]{2,1,0:T(8,128)S(1)} collective-permute-done((f32[5,16,768]{2,1,0:T(8,128)S(1)}, f32[5,16,768]{2,1,0:T(8,128)S(1)}, u32[]{:S(2)}, u32[]{:S(2)}) %collective-permute-start.25) | collective-permute-done | bytes 245792 | tf_op jit(solution)/shard_map/ppermute | solution.py:290
  240.0 2.0 collective-permute-start.26
  242.0 2.3 collective-permute-start.27
  244.3 4.8 %collective-permute-done.27.high_ref = f32[5,8,768]{2,1,0:T(8,128)S(1)} collective-permute-done((f32[5,8,768]{2,1,0:T(8,128)S(1)}, f32[5,8,768]{2,1,0:T(8,128)S(1)}, u32[]{:S(2)}, u32[]{:S(2)}) %collective-permute-start.27) | collective-permute-done | bytes 122912 | tf_op jit(solution)/shard_map/ppermute | solution.py:290
  249.5 1.9 collective-permute-start.28
  251.4 2.4 collective-permute-start.29
  253.9 4.7 %collective-permute-done.29.high_ref = f32[5,8,768]{2,1,0:T(8,128)S(1)} collective-permute-done((f32[5,8,768]{2,1,0:T(8,128)S(1)}, f32[5,8,768]{2,1,0:T(8,128)S(1)}, u32[]{:S(2)}, u32[]{:S(2)}) %collective-permute-start.29) | collective-permute-done | bytes 122912 | tf_op jit(solution)/shard_map/ppermute | solution.py:290
  258.9 5.1 %collective-permute-start.30 = (f32[5,16,768]{2,1,0:T(8,128)S(1)}, f32[5,16,768]{2,1,0:T(8,128)S(1)}, u32[]{:S(2)}, u32[]{:S(2)}) collective-permute-start(f32[5,16,768]{2,1,0:T(8,128)S(1)} %get-tuple-element.120), channel_id=1, source_target_pairs={{0,1},{1,2},{2,3},{3,4},{4,5},{5,6},{6,7},{7,8},{8,9},{9,10},{10,1... | collective-permute-start | bytes 737288 | tf_op jit(solution)/shard_map/ppermute | solution.py:289
  264.0 1.9 collective-permute-start.31
  265.9 8.1 %collective-permute-done.30.refs_0_ = f32[5,16,768]{2,1,0:T(8,128)S(1)} collective-permute-done((f32[5,16,768]{2,1,0:T(8,128)S(1)}, f32[5,16,768]{2,1,0:T(8,128)S(1)}, u32[]{:S(2)}, u32[]{:S(2)}) %collective-permute-start.30) | collective-permute-done | bytes 245792 | tf_op jit(solution)/shard_map/ppermute | solution.py:289
  274.1 6.2 %collective-permute-done.31.refs_2_ = f32[5,16,768]{2,1,0:T(8,128)S(1)} collective-permute-done((f32[5,16,768]{2,1,0:T(8,128)S(1)}, f32[5,16,768]{2,1,0:T(8,128)S(1)}, u32[]{:S(2)}, u32[]{:S(2)}) %collective-permute-start.31) | collective-permute-done | bytes 245792 | tf_op jit(solution)/shard_map/ppermute | solution.py:290
  280.3 1.9 update.7
  (35 shorter events, 17.4 us)
Async XLA Ops:
  0.0 0.7 copy-start.2
  0.7 0.7 copy-start.3
  2.9 1.0 copy-start
  3.9 42.7 %copy-start.4 = (f32[8,24,512]{2,1,0:T(8,128)S(1)}, f32[8,24,512]{2,1,0:T(8,128)}, u32[]{:S(2)}) copy-start(f32[8,24,512]{2,1,0:T(8,128)} %param.6) | copy-start | bytes 1179652
  4.8 15.1 %collective-permute-start = (f32[5,16,768]{2,1,0:T(8,128)S(1)}, f32[5,16,768]{2,1,0:T(8,128)S(1)}, u32[]{:S(2)}, u32[]{:S(2)}) collective-permute-start(f32[5,16,768]{2,1,0:T(8,128)S(1)} %get-tuple-element.70), channel_id=1, source_target_pairs={{0,1},{1,2},{2,3},{3,4},{4,5},{5,6},{6,7},{7,8},{8,9},{9,10},{10,1... | collective-permute-start | bytes 737288 | tf_op jit(solution)/shard_map/ppermute | solution.py:289
  8.1 13.2 %collective-permute-start.1 = (f32[5,16,768]{2,1,0:T(8,128)S(1)}, f32[5,16,768]{2,1,0:T(8,128)S(1)}, u32[]{:S(2)}, u32[]{:S(2)}) collective-permute-start(f32[5,16,768]{2,1,0:T(8,128)S(1)} %get-tuple-element.72), channel_id=1, source_target_pairs={{1,0},{2,1},{3,2},{4,3},{5,4},{6,5},{7,6},{8,7},{9,8},{10,9},{11,1... | collective-permute-start | bytes 737288 | tf_op jit(solution)/shard_map/ppermute | solution.py:290
  21.7 16.7 %collective-permute-start.2 = (f32[15,8,768]{2,1,0:T(8,128)S(1)}, f32[15,8,768]{2,1,0:T(8,128)S(1)}, u32[]{:S(2)}, u32[]{:S(2)}) collective-permute-start(f32[15,8,768]{2,1,0:T(8,128)S(1)} %get-tuple-element.73), channel_id=1, source_target_pairs={{0,16},{16,32},{32,48},{48,64},{64,80},{80,96},{96,112},{112,128},... | collective-permute-start | bytes 1105928 | tf_op jit(solution)/shard_map/ppermute | solution.py:289
  30.8 9.7 %collective-permute-start.3 = (f32[15,8,768]{2,1,0:T(8,128)S(1)}, f32[15,8,768]{2,1,0:T(8,128)S(1)}, u32[]{:S(2)}, u32[]{:S(2)}) collective-permute-start(f32[15,8,768]{2,1,0:T(8,128)S(1)} %get-tuple-element.75), channel_id=1, source_target_pairs={{16,0},{32,16},{48,32},{64,48},{80,64},{96,80},{112,96},{128,112},... | collective-permute-start | bytes 1105928 | tf_op jit(solution)/shard_map/ppermute | solution.py:290
  41.6 25.3 %collective-permute-start.4 = (f32[15,8,768]{2,1,0:T(8,128)S(1)}, f32[15,8,768]{2,1,0:T(8,128)S(1)}, u32[]{:S(2)}, u32[]{:S(2)}) collective-permute-start(f32[15,8,768]{2,1,0:T(8,128)S(1)} %get-tuple-element.76), channel_id=1, source_target_pairs={{0,16},{16,32},{32,48},{48,64},{64,80},{80,96},{96,112},{112,128},... | collective-permute-start | bytes 1105928 | tf_op jit(solution)/shard_map/ppermute | solution.py:289
  44.7 22.2 %collective-permute-start.5 = (f32[15,8,768]{2,1,0:T(8,128)S(1)}, f32[15,8,768]{2,1,0:T(8,128)S(1)}, u32[]{:S(2)}, u32[]{:S(2)}) collective-permute-start(f32[15,8,768]{2,1,0:T(8,128)S(1)} %get-tuple-element.78), channel_id=1, source_target_pairs={{16,0},{32,16},{48,32},{64,48},{80,64},{96,80},{112,96},{128,112},... | collective-permute-start | bytes 1105928 | tf_op jit(solution)/shard_map/ppermute | solution.py:290
  52.6 37.3 %copy-start.1 = (f32[8,16,768]{2,1,0:T(8,128)S(1)}, f32[8,16,768]{2,1,0:T(8,128)}, u32[]{:S(2)}) copy-start(f32[8,16,768]{2,1,0:T(8,128)} %estimate_ref.3) | copy-start | bytes 1179652
  55.3 60.3 %all-to-all-start = ((f32[32,24,128]{2,1,0:T(8,128)}), f32[32,24,128]{2,1,0:T(8,128)}, u32[]{:S(2)}, u32[]{:S(2)}) async-start(f32[32,24,128]{2,1,0:T(8,128)} %copy.13), calls=%async_computation | async-start | bytes 786432 | tf_op jit(solution)/shard_map/all_to_all | solution.py:299
  67.9 15.6 %collective-permute-start.6 = (f32[5,16,768]{2,1,0:T(8,128)S(1)}, f32[5,16,768]{2,1,0:T(8,128)S(1)}, u32[]{:S(2)}, u32[]{:S(2)}) collective-permute-start(f32[5,16,768]{2,1,0:T(8,128)S(1)} %get-tuple-element.79), channel_id=1, source_target_pairs={{0,1},{1,2},{2,3},{3,4},{4,5},{5,6},{6,7},{7,8},{8,9},{9,10},{10,1... | collective-permute-start | bytes 737288 | tf_op jit(solution)/shard_map/ppermute | solution.py:289
  72.2 17.7 %collective-permute-start.7 = (f32[5,16,768]{2,1,0:T(8,128)S(1)}, f32[5,16,768]{2,1,0:T(8,128)S(1)}, u32[]{:S(2)}, u32[]{:S(2)}) collective-permute-start(f32[5,16,768]{2,1,0:T(8,128)S(1)} %get-tuple-element.81), channel_id=1, source_target_pairs={{1,0},{2,1},{3,2},{4,3},{5,4},{6,5},{7,6},{8,7},{9,8},{10,9},{11,1... | collective-permute-start | bytes 737288 | tf_op jit(solution)/shard_map/ppermute | solution.py:290
  91.7 15.2 %collective-permute-start.8 = (f32[5,16,768]{2,1,0:T(8,128)S(1)}, f32[5,16,768]{2,1,0:T(8,128)S(1)}, u32[]{:S(2)}, u32[]{:S(2)}) collective-permute-start(f32[5,16,768]{2,1,0:T(8,128)S(1)} %get-tuple-element.85), channel_id=1, source_target_pairs={{0,1},{1,2},{2,3},{3,4},{4,5},{5,6},{6,7},{7,8},{8,9},{9,10},{10,1... | collective-permute-start | bytes 737288 | tf_op jit(solution)/shard_map/ppermute | solution.py:289
  93.6 17.3 %collective-permute-start.9 = (f32[5,16,768]{2,1,0:T(8,128)S(1)}, f32[5,16,768]{2,1,0:T(8,128)S(1)}, u32[]{:S(2)}, u32[]{:S(2)}) collective-permute-start(f32[5,16,768]{2,1,0:T(8,128)S(1)} %get-tuple-element.87), channel_id=1, source_target_pairs={{1,0},{2,1},{3,2},{4,3},{5,4},{6,5},{7,6},{8,7},{9,8},{10,9},{11,1... | collective-permute-start | bytes 737288 | tf_op jit(solution)/shard_map/ppermute | solution.py:290
  111.3 5.5 %collective-permute-start.10 = (f32[5,8,768]{2,1,0:T(8,128)S(1)}, f32[5,8,768]{2,1,0:T(8,128)S(1)}, u32[]{:S(2)}, u32[]{:S(2)}) collective-permute-start(f32[5,8,768]{2,1,0:T(8,128)S(1)} %get-tuple-element.88), channel_id=1, source_target_pairs={{0,16},{16,32},{32,48},{48,64},{64,80},{80,96},{96,112},{112,128},... | collective-permute-start | bytes 368648 | tf_op jit(solution)/shard_map/ppermute | solution.py:289
  113.2 7.1 %collective-permute-start.11 = (f32[5,8,768]{2,1,0:T(8,128)S(1)}, f32[5,8,768]{2,1,0:T(8,128)S(1)}, u32[]{:S(2)}, u32[]{:S(2)}) collective-permute-start(f32[5,8,768]{2,1,0:T(8,128)S(1)} %get-tuple-element.90), channel_id=1, source_target_pairs={{16,0},{32,16},{48,32},{64,48},{80,64},{96,80},{112,96},{128,112},... | collective-permute-start | bytes 368648 | tf_op jit(solution)/shard_map/ppermute | solution.py:290
  120.7 4.3 %collective-permute-start.12 = (f32[5,8,768]{2,1,0:T(8,128)S(1)}, f32[5,8,768]{2,1,0:T(8,128)S(1)}, u32[]{:S(2)}, u32[]{:S(2)}) collective-permute-start(f32[5,8,768]{2,1,0:T(8,128)S(1)} %get-tuple-element.91), channel_id=1, source_target_pairs={{0,16},{16,32},{32,48},{48,64},{64,80},{80,96},{96,112},{112,128},... | collective-permute-start | bytes 368648 | tf_op jit(solution)/shard_map/ppermute | solution.py:289
  122.6 7.1 %collective-permute-start.13 = (f32[5,8,768]{2,1,0:T(8,128)S(1)}, f32[5,8,768]{2,1,0:T(8,128)S(1)}, u32[]{:S(2)}, u32[]{:S(2)}) collective-permute-start(f32[5,8,768]{2,1,0:T(8,128)S(1)} %get-tuple-element.93), channel_id=1, source_target_pairs={{16,0},{32,16},{48,32},{64,48},{80,64},{96,80},{112,96},{128,112},... | collective-permute-start | bytes 368648 | tf_op jit(solution)/shard_map/ppermute | solution.py:290
  130.1 14.8 %collective-permute-start.14 = (f32[5,16,768]{2,1,0:T(8,128)S(1)}, f32[5,16,768]{2,1,0:T(8,128)S(1)}, u32[]{:S(2)}, u32[]{:S(2)}) collective-permute-start(f32[5,16,768]{2,1,0:T(8,128)S(1)} %get-tuple-element.94), channel_id=1, source_target_pairs={{0,1},{1,2},{2,3},{3,4},{4,5},{5,6},{6,7},{7,8},{8,9},{9,10},{10,1... | collective-permute-start | bytes 737288 | tf_op jit(solution)/shard_map/ppermute | solution.py:289
  132.1 15.9 %collective-permute-start.15 = (f32[5,16,768]{2,1,0:T(8,128)S(1)}, f32[5,16,768]{2,1,0:T(8,128)S(1)}, u32[]{:S(2)}, u32[]{:S(2)}) collective-permute-start(f32[5,16,768]{2,1,0:T(8,128)S(1)} %get-tuple-element.96), channel_id=1, source_target_pairs={{1,0},{2,1},{3,2},{4,3},{5,4},{6,5},{7,6},{8,7},{9,8},{10,9},{11,1... | collective-permute-start | bytes 737288 | tf_op jit(solution)/shard_map/ppermute | solution.py:290
  149.7 14.0 %collective-permute-start.16 = (f32[5,16,768]{2,1,0:T(8,128)S(1)}, f32[5,16,768]{2,1,0:T(8,128)S(1)}, u32[]{:S(2)}, u32[]{:S(2)}) collective-permute-start(f32[5,16,768]{2,1,0:T(8,128)S(1)} %get-tuple-element.98), channel_id=1, source_target_pairs={{0,1},{1,2},{2,3},{3,4},{4,5},{5,6},{6,7},{7,8},{8,9},{9,10},{10,1... | collective-permute-start | bytes 737288 | tf_op jit(solution)/shard_map/ppermute | solution.py:289
  151.6 18.0 %collective-permute-start.17 = (f32[5,16,768]{2,1,0:T(8,128)S(1)}, f32[5,16,768]{2,1,0:T(8,128)S(1)}, u32[]{:S(2)}, u32[]{:S(2)}) collective-permute-start(f32[5,16,768]{2,1,0:T(8,128)S(1)} %get-tuple-element.100), channel_id=1, source_target_pairs={{1,0},{2,1},{3,2},{4,3},{5,4},{6,5},{7,6},{8,7},{9,8},{10,9},{11,1... | collective-permute-start | bytes 737288 | tf_op jit(solution)/shard_map/ppermute | solution.py:290
  170.1 9.3 %collective-permute-start.18 = (f32[15,8,768]{2,1,0:T(8,128)S(1)}, f32[15,8,768]{2,1,0:T(8,128)S(1)}, u32[]{:S(2)}, u32[]{:S(2)}) collective-permute-start(f32[15,8,768]{2,1,0:T(8,128)S(1)} %get-tuple-element.101), channel_id=1, source_target_pairs={{0,16},{16,32},{32,48},{48,64},{64,80},{80,96},{96,112},{112,128},... | collective-permute-start | bytes 1105928 | tf_op jit(solution)/shard_map/ppermute | solution.py:289
  173.7 9.7 %collective-permute-start.19 = (f32[15,8,768]{2,1,0:T(8,128)S(1)}, f32[15,8,768]{2,1,0:T(8,128)S(1)}, u32[]{:S(2)}, u32[]{:S(2)}) collective-permute-start(f32[15,8,768]{2,1,0:T(8,128)S(1)} %get-tuple-element.103), channel_id=1, source_target_pairs={{16,0},{32,16},{48,32},{64,48},{80,64},{96,80},{112,96},{128,112},... | collective-permute-start | bytes 1105928 | tf_op jit(solution)/shard_map/ppermute | solution.py:290
  184.4 7.3 %collective-permute-start.20 = (f32[15,8,768]{2,1,0:T(8,128)S(1)}, f32[15,8,768]{2,1,0:T(8,128)S(1)}, u32[]{:S(2)}, u32[]{:S(2)}) collective-permute-start(f32[15,8,768]{2,1,0:T(8,128)S(1)} %get-tuple-element.104), channel_id=1, source_target_pairs={{0,16},{16,32},{32,48},{48,64},{64,80},{80,96},{96,112},{112,128},... | collective-permute-start | bytes 1105928 | tf_op jit(solution)/shard_map/ppermute | solution.py:289
  186.4 11.1 %collective-permute-start.21 = (f32[15,8,768]{2,1,0:T(8,128)S(1)}, f32[15,8,768]{2,1,0:T(8,128)S(1)}, u32[]{:S(2)}, u32[]{:S(2)}) collective-permute-start(f32[15,8,768]{2,1,0:T(8,128)S(1)} %get-tuple-element.106), channel_id=1, source_target_pairs={{16,0},{32,16},{48,32},{64,48},{80,64},{96,80},{112,96},{128,112},... | collective-permute-start | bytes 1105928 | tf_op jit(solution)/shard_map/ppermute | solution.py:290
  198.4 14.3 %collective-permute-start.22 = (f32[5,16,768]{2,1,0:T(8,128)S(1)}, f32[5,16,768]{2,1,0:T(8,128)S(1)}, u32[]{:S(2)}, u32[]{:S(2)}) collective-permute-start(f32[5,16,768]{2,1,0:T(8,128)S(1)} %get-tuple-element.107), channel_id=1, source_target_pairs={{0,1},{1,2},{2,3},{3,4},{4,5},{5,6},{6,7},{7,8},{8,9},{9,10},{10,1... | collective-permute-start | bytes 737288 | tf_op jit(solution)/shard_map/ppermute | solution.py:289
  200.3 16.0 %collective-permute-start.23 = (f32[5,16,768]{2,1,0:T(8,128)S(1)}, f32[5,16,768]{2,1,0:T(8,128)S(1)}, u32[]{:S(2)}, u32[]{:S(2)}) collective-permute-start(f32[5,16,768]{2,1,0:T(8,128)S(1)} %get-tuple-element.109), channel_id=1, source_target_pairs={{1,0},{2,1},{3,2},{4,3},{5,4},{6,5},{7,6},{8,7},{9,8},{10,9},{11,1... | collective-permute-start | bytes 737288 | tf_op jit(solution)/shard_map/ppermute | solution.py:290
  218.1 15.8 %collective-permute-start.24 = (f32[5,16,768]{2,1,0:T(8,128)S(1)}, f32[5,16,768]{2,1,0:T(8,128)S(1)}, u32[]{:S(2)}, u32[]{:S(2)}) collective-permute-start(f32[5,16,768]{2,1,0:T(8,128)S(1)} %get-tuple-element.111), channel_id=1, source_target_pairs={{0,1},{1,2},{2,3},{3,4},{4,5},{5,6},{6,7},{7,8},{8,9},{9,10},{10,1... | collective-permute-start | bytes 737288 | tf_op jit(solution)/shard_map/ppermute | solution.py:289
  223.7 15.9 %collective-permute-start.25 = (f32[5,16,768]{2,1,0:T(8,128)S(1)}, f32[5,16,768]{2,1,0:T(8,128)S(1)}, u32[]{:S(2)}, u32[]{:S(2)}) collective-permute-start(f32[5,16,768]{2,1,0:T(8,128)S(1)} %get-tuple-element.113), channel_id=1, source_target_pairs={{1,0},{2,1},{3,2},{4,3},{5,4},{6,5},{7,6},{8,7},{9,8},{10,9},{11,1... | collective-permute-start | bytes 737288 | tf_op jit(solution)/shard_map/ppermute | solution.py:290
  240.0 4.3 %collective-permute-start.26 = (f32[5,8,768]{2,1,0:T(8,128)S(1)}, f32[5,8,768]{2,1,0:T(8,128)S(1)}, u32[]{:S(2)}, u32[]{:S(2)}) collective-permute-start(f32[5,8,768]{2,1,0:T(8,128)S(1)} %get-tuple-element.114), channel_id=1, source_target_pairs={{0,16},{16,32},{32,48},{48,64},{64,80},{80,96},{96,112},{112,128},... | collective-permute-start | bytes 368648 | tf_op jit(solution)/shard_map/ppermute | solution.py:289
  242.0 7.1 %collective-permute-start.27 = (f32[5,8,768]{2,1,0:T(8,128)S(1)}, f32[5,8,768]{2,1,0:T(8,128)S(1)}, u32[]{:S(2)}, u32[]{:S(2)}) collective-permute-start(f32[5,8,768]{2,1,0:T(8,128)S(1)} %get-tuple-element.116), channel_id=1, source_target_pairs={{16,0},{32,16},{48,32},{64,48},{80,64},{96,80},{112,96},{128,112},... | collective-permute-start | bytes 368648 | tf_op jit(solution)/shard_map/ppermute | solution.py:290
  249.5 4.3 %collective-permute-start.28 = (f32[5,8,768]{2,1,0:T(8,128)S(1)}, f32[5,8,768]{2,1,0:T(8,128)S(1)}, u32[]{:S(2)}, u32[]{:S(2)}) collective-permute-start(f32[5,8,768]{2,1,0:T(8,128)S(1)} %get-tuple-element.117), channel_id=1, source_target_pairs={{0,16},{16,32},{32,48},{48,64},{64,80},{80,96},{96,112},{112,128},... | collective-permute-start | bytes 368648 | tf_op jit(solution)/shard_map/ppermute | solution.py:289
  251.4 7.1 %collective-permute-start.29 = (f32[5,8,768]{2,1,0:T(8,128)S(1)}, f32[5,8,768]{2,1,0:T(8,128)S(1)}, u32[]{:S(2)}, u32[]{:S(2)}) collective-permute-start(f32[5,8,768]{2,1,0:T(8,128)S(1)} %get-tuple-element.119), channel_id=1, source_target_pairs={{16,0},{32,16},{48,32},{64,48},{80,64},{96,80},{112,96},{128,112},... | collective-permute-start | bytes 368648 | tf_op jit(solution)/shard_map/ppermute | solution.py:290
  258.9 15.1 %collective-permute-start.30 = (f32[5,16,768]{2,1,0:T(8,128)S(1)}, f32[5,16,768]{2,1,0:T(8,128)S(1)}, u32[]{:S(2)}, u32[]{:S(2)}) collective-permute-start(f32[5,16,768]{2,1,0:T(8,128)S(1)} %get-tuple-element.120), channel_id=1, source_target_pairs={{0,1},{1,2},{2,3},{3,4},{4,5},{5,6},{6,7},{7,8},{8,9},{9,10},{10,1... | collective-permute-start | bytes 737288 | tf_op jit(solution)/shard_map/ppermute | solution.py:289
  264.0 16.2 %collective-permute-start.31 = (f32[5,16,768]{2,1,0:T(8,128)S(1)}, f32[5,16,768]{2,1,0:T(8,128)S(1)}, u32[]{:S(2)}, u32[]{:S(2)}) collective-permute-start(f32[5,16,768]{2,1,0:T(8,128)S(1)} %get-tuple-element.122), channel_id=1, source_target_pairs={{1,0},{2,1},{3,2},{4,3},{5,4},{6,5},{7,6},{8,7},{9,8},{10,9},{11,1... | collective-permute-start | bytes 737288 | tf_op jit(solution)/shard_map/ppermute | solution.py:290
